TPU v7x, 32 devices: a whole 2x2x4 slice. The times are simulated.
32 devices in a mesh: dom: 16 (over z, y, x), segment: 2 (over core).
Axes of the slice: x: 2, y: 2, z: 4, core: 2. Of those that a mesh axis runs over, the one named last changes fastest.
Arguments:
- feats: bfloat16 [4096, 512], P('dom'), may hold values from -6 to 6
- adj_local: bfloat16 [4096, 256], P('dom'), as said below
- couple: bfloat16 [4096, 256], P('dom'), as said below
- send_rows: int32 [16, 256], P('dom'), may hold values from 0 to 255, as said below
- weights: bfloat16 [1024, 512], P('segment'), may hold values from -0.25 to 0.25
- cotangent: bfloat16 [4096, 512], P('dom'), may hold values from -1.5 to 1.5
Outputs:
- acts: bfloat16 [2, 4096, 512], P('segment', 'dom')
- grad_weights: float32 [2, 512, 512], P('segment', 'dom')
- grad_feats: float32 [4096, 512], P('dom', 'segment')
Inputs may be any that keep to these rules, and one draw needn't show every extreme that they name: `adj_local`: entries are non-negative. `couple`: entries are non-negative. `send_rows`: the 128 local indices that a partition sends in one round are distinct.
All inputs are finite; a program needn't handle non-finite values.
Results may differ from a plain program's by a relative error of at most 0.013.
Values may be sent and summed in bfloat16 or wider, within the bound.
No kernel may reach another device: no remote copies, remote signals or barrier semaphores. Data moves between devices by JAX's collectives and lax.ppermute only.
A program may use at most 64 MiB of HBM per device.

v0:
```python
import math

import jax
import jax.numpy as jnp
from jax import lax
from jax.experimental import pallas as pl
from jax.experimental.pallas import tpu as pltpu
from jax.sharding import PartitionSpec as P


SHARE = 0.1
BETA_SCALE = 0.5
BF16 = jnp.bfloat16
F32 = jnp.float32


def swapped(x, mask):
    return lax.ppermute(x, "dom", [(i, i ^ mask) for i in range(lax.axis_size("dom"))])


def every_piece(x):
    n = lax.axis_size("segment")
    return [x] + [lax.ppermute(x, "segment", [(i, (i + k) % n) for i in range(n)]) for k in range(1, n)]


def beta_of(k):
    return math.log(BETA_SCALE / (k + 1.0) + 1.0)


def mm(a, b):
    return jnp.dot(a, b, preferred_element_type=F32)


def mm_nt(a, b):
    return lax.dot_general(a, b, (((1,), (1,)), ((), ())), preferred_element_type=F32)


def mm_tn(a, b):
    return lax.dot_general(a, b, (((0,), (0,)), ((), ())), preferred_element_type=F32)


def position():
    n = lax.axis_size("dom")
    dom = lax.axis_index("dom")
    return lax.axis_index("segment"), lax.rem(dom, 2), lax.div(dom, n // 2), lax.rem(lax.div(dom, 2), n // 4)


def place_of(seg, k, n):
    return lax.rem(seg - k + n, n)


def in_hbm(x):
    return pltpu.with_memory_space_constraint(x, pltpu.HBM)


def call(body, out_shape, ins, scratch=(), vmem=20):
    spaces = {"h": pltpu.HBM, "v": pltpu.VMEM}
    specs = [pl.BlockSpec(memory_space=spaces[m]) for _, m in ins]
    arrays = [in_hbm(a) if m == "h" else a for a, m in ins]
    return pl.pallas_call(
        body,
        out_shape=tuple(out_shape),
        in_specs=specs,
        out_specs=tuple(pl.BlockSpec(memory_space=pltpu.VMEM) for _ in out_shape),
        scratch_shapes=list(scratch),
        compiler_params=pltpu.CompilerParams(vmem_limit_bytes=vmem << 20),
    )(*arrays)


sds = jax.ShapeDtypeStruct


def pack_call(feats, adj, couple, send_rows, cot, layers):
    rows, width = feats.shape
    piece = rows // layers
    picked = send_rows.shape[1]

    def body(feats_r, adj_r, couple_r, sr_r, cot_r, fwd_o, cot_o, sr_s, sems):
        at = pl.ds(pl.multiple_of(lax.axis_index("segment") * piece, piece), piece)
        split = adj_r.shape[1]
        copies = [
            pltpu.make_async_copy(adj_r.at[at, :], fwd_o.at[:piece, :split], sems.at[1]),
            pltpu.make_async_copy(couple_r.at[at, :], fwd_o.at[:piece, split:], sems.at[2]),
            pltpu.make_async_copy(feats_r.at[at, :], fwd_o.at[piece : 2 * piece, :], sems.at[0]),
            pltpu.make_async_copy(cot_r.at[at, :], cot_o, sems.at[3]),
        ]
        sr_copy = pltpu.make_async_copy(sr_r, sr_s, sems.at[4])
        sr_copy.start()
        for c in copies:
            c.start()
        fwd_o[2 * piece :, picked:] = jnp.zeros((8, width - picked), BF16)
        sr_copy.wait()
        fwd_o[2 * piece :, :picked] = jnp.broadcast_to(sr_s[...].astype(F32), (8, picked)).astype(BF16)
        for c in copies:
            c.wait()

    return call(
        body,
        (sds((2 * piece + 8, width), BF16), sds((piece, width), BF16)),
        [(feats, "h"), (adj, "h"), (couple, "h"), (send_rows, "h"), (cot, "h")],
        [pltpu.VMEM(send_rows.shape, jnp.int32), pltpu.SemaphoreType.DMA((5,))],
        4,
    )


def picks_of(sr, rows):
    ids = lax.broadcasted_iota(jnp.int32, (rows, sr.shape[1]), 0).astype(F32)
    return (ids == sr).astype(F32).astype(BF16)


def scaled(first):
    return SHARE * first.astype(F32)


def mixed_of(agg, first_scaled):
    return ((1.0 - SHARE) * agg + first_scaled).astype(BF16)


def activate(mixed, w, k):
    beta = beta_of(k)
    half = (0.5 - 0.5 * beta) * mixed.astype(F32) + (0.5 * beta) * mm(mixed, w)
    t = jnp.tanh(half)
    up = 1.0 + t
    return up * (1.0 + half * (1.0 - t)), (half * up).astype(BF16)


def along(dim, *parts):
    return jnp.concatenate(parts, axis=dim)


def piece_slice(seg, k, layers, piece):
    return pl.ds(pl.multiple_of(place_of(seg, k, layers) * piece, piece), piece)


def prep_call(feats, adj, couple, send_rows):
    rows, width = feats.shape

    def body(feats_r, adj_r, couple_r, sr_r, x_o, own_o, couple_o, pick_o, agg_o, sr_s, sems):
        copies = [
            pltpu.make_async_copy(sr_r, sr_s, sems.at[0]),
            pltpu.make_async_copy(couple_r, couple_o, sems.at[1]),
            pltpu.make_async_copy(feats_r, x_o, sems.at[2]),
            pltpu.make_async_copy(adj_r, own_o, sems.at[3]),
        ]
        for c in copies:
            c.start()
        for c in copies:
            c.wait()
        pick_o[...] = picks_of(sr_s[...].astype(F32), rows)
        agg_o[...] = mm(own_o[...], x_o[...])

    return call(
        body,
        (
            sds((rows, width), BF16),
            sds((rows, rows), BF16),
            sds((rows, couple.shape[1]), BF16),
            sds((rows, send_rows.shape[1]), BF16),
            sds((rows, width), F32),
        ),
        [(feats, "h"), (adj, "h"), (couple, "h"), (send_rows, "h")],
        [pltpu.VMEM(send_rows.shape, jnp.int32), pltpu.SemaphoreType.DMA((4,))],
        8,
    )


def own_call(near, far, w_pieces, prep):
    x, _, couple, pick, agg = prep
    layers = len(near)
    rows, width = x.shape
    piece = rows // layers
    bound = couple.shape[1] // 2

    def body(x_r, couple_r, pick_r, agg_r, *refs):
        got_r = [refs[g * layers : (g + 1) * layers] for g in range(2)]
        w_r = refs[2 * layers : 3 * layers]
        outs = refs[3 * layers :]
        x12_o, mix_o, slope_o, x1_o, sums_o, own12_o, near01_o, far02_o, cp_o, pick_o, w_o, first_o, ac_s, sem = outs
        seg = lax.axis_index("segment")
        w_copy = pltpu.make_async_copy(w_r[0], w_o.at[seg], sem)
        w_copy.start()
        for k in range(1, layers):
            w_o[place_of(seg, k, layers)] = w_r[k][...]
        picks = []
        for g in range(2):
            for k in range(layers):
                at = piece_slice(seg, k, layers, piece)
                own12_o[g, at, :] = got_r[g][k][:piece, :rows]
                ac_s[g, at, :] = got_r[g][k][:piece, rows:]
                x12_o[g, at, :] = got_r[g][k][piece : 2 * piece, :]
            picks.append(picks_of(got_r[g][0][2 * piece : 2 * piece + 1, : 2 * bound].astype(F32), rows))
        near01_o[0] = mm_nt(couple_r[:, :bound], picks[0][:, :bound]).astype(BF16)
        far02_o[0] = mm_nt(couple_r[:, bound:], picks[1][:, bound:]).astype(BF16)
        near01_o[1] = mm_nt(ac_s[0, :, :bound], pick_r[:, :bound]).astype(BF16)
        far02_o[1] = mm_nt(ac_s[1, :, bound:], pick_r[:, bound:]).astype(BF16)
        cp_o[0] = ac_s[0, :, bound:]
        cp_o[1] = ac_s[1, :, :bound]
        pick_o[0] = picks[0][:, bound:]
        pick_o[1] = picks[1][:, :bound]
        sums_o[0] = mm(along(1, own12_o[0], near01_o[1]), along(0, x12_o[0], x_r[...]))
        sums_o[1] = mm(along(1, own12_o[1], far02_o[1]), along(0, x12_o[1], x_r[...]))
        first_o[0] = scaled(x_r[...])
        first_o[1] = scaled(x12_o[0])
        first_o[2] = scaled(x12_o[1])
        w_copy.wait()
        agg = agg_r[...] + mm(along(1, near01_o[0], far02_o[0]), along(0, x12_o[0], x12_o[1]))
        mixed = mixed_of(agg, first_o[0])
        mix_o[...] = mixed
        slope_o[...], x1_o[...] = activate(mixed, w_o[0], 0)

    return call(
        body,
        (
            sds((2, rows, width), BF16),
            sds((rows, width), BF16),
            sds((rows, width), F32),
            sds((rows, width), BF16),
            sds((2, rows, width), F32),
            sds((2, rows, rows), BF16),
            sds((2, rows, rows), BF16),
            sds((2, rows, rows), BF16),
            sds((2, rows, bound), BF16),
            sds((2, rows, bound), BF16),
            sds((layers, width, width), BF16),
            sds((3, rows, width), F32),
        ),
        [(a, "v") for a in (x, couple, pick, agg, *near, *far)]
        + [(w_pieces[0], "h")]
        + [(w, "v") for w in w_pieces[1:]],
        [pltpu.VMEM((2, rows, 2 * bound), BF16), pltpu.SemaphoreType.DMA],
        14 + 2 * layers,
    )


def rest_call(diag, own):
    x12, _, _, _, sums, _, _, _, cp, pick, w, first = own
    layers = len(diag)
    _, rows, width = x12.shape
    piece = rows // layers
    bound = cp.shape[2]

    def body(x12_r, sums_r, cp_r, pick_r, w_r, first_r, *refs):
        got_r = refs[:layers]
        first3_o, x3_s, mix_o, slope_o, x1_o, own3_o, near23_o, far13_o, ac_s = (refs[layers], refs[-1], *refs[layers + 1 : -1])
        seg = lax.axis_index("segment")
        for k in range(layers):
            at = piece_slice(seg, k, layers, piece)
            own3_o[at, :] = got_r[k][:piece, :rows]
            ac_s[at, :] = got_r[k][:piece, rows:]
            x3_s[at, :] = got_r[k][piece : 2 * piece, :]
        first3_o[...] = scaled(x3_s[...])
        picks = picks_of(got_r[0][2 * piece : 2 * piece + 1, : 2 * bound].astype(F32), rows)
        far13_o[0] = mm_nt(cp_r[0], picks[:, bound:]).astype(BF16)
        near23_o[0] = mm_nt(cp_r[1], picks[:, :bound]).astype(BF16)
        near23_o[1] = mm_nt(ac_s[:, :bound], pick_r[1]).astype(BF16)
        far13_o[1] = mm_nt(ac_s[:, bound:], pick_r[0]).astype(BF16)
        for g in range(3):
            if g < 2:
                agg = sums_r[g] + mm((far13_o, near23_o)[g][0], x3_s[...])
            else:
                agg = mm(along(1, own3_o[...], near23_o[1], far13_o[1]), along(0, x3_s[...], x12_r[1], x12_r[0]))
            mixed = mixed_of(agg, first_r[g + 1] if g < 2 else first3_o[...])
            mix_o[g] = mixed
            slope_o[g], x1_o[g] = activate(mixed, w_r[0], 0)

    return call(
        body,
        (
            sds((rows, width), F32),
            sds((3, rows, width), BF16),
            sds((3, rows, width), F32),
            sds((3, rows, width), BF16),
            sds((rows, rows), BF16),
            sds((2, rows, rows), BF16),
            sds((2, rows, rows), BF16),
        ),
        [(a, "v") for a in (x12, sums, cp, pick, w, first, *diag)],
        [pltpu.VMEM((rows, 2 * bound), BF16), pltpu.VMEM((rows, width), BF16)],
        16,
    )


def matrix_of(prep, own, rest):
    arrays = (prep[1], own[5], rest[4], own[6], rest[5], own[7], rest[6])

    def readers(refs):
        own0, own12, own3, near01, near23, far02, far13 = refs
        return (
            lambda g: own0[...] if g == 0 else own3[...] if g == 3 else own12[g - 1],
            lambda g: (near01, near23)[g // 2][g % 2],
            lambda g: (far02, far13)[g % 2][g // 2],
        )

    return arrays, readers


def later_call(w, own, rest, matrix):
    arrays, readers = matrix
    layers = w.shape[0]
    rows, width = own[1].shape
    m = len(arrays)

    def body(first_r, first3_r, x1_r, x1n_r, w_r, *refs):
        own_at, near_at, far_at = readers(refs[:m])
        acts_o, mix_o, slope_o, xa_s, xb_s = refs[m:]
        seg = lax.axis_index("segment")

        @pl.when(seg == 0)
        def _():
            acts_o[...] = x1_r[...]

        def src(g):
            return x1n_r[g - 1] if g else x1_r[...]

        for k in range(1, layers):
            dst = (xa_s, xb_s)[k % 2]
            for g in range(4):
                agg = mm(along(1, own_at(g), near_at(g), far_at(g)), along(0, src(g), src(g ^ 1), src(g ^ 2)))
                mixed = mixed_of(agg, first_r[g] if g < 3 else first3_r[...])
                mix_o[k - 1, g] = mixed
                slope_o[k - 1, g], out = activate(mixed, w_r[k], k)
                if k + 1 < layers:
                    dst[g] = out
                if g == 0:

                    @pl.when(seg == k)
                    def _():
                        acts_o[...] = out

            def src(g, dst=dst):
                return dst[g]

    return call(
        body,
        (
            sds((rows, width), BF16),
            sds((layers - 1, 4, rows, width), BF16),
            sds((layers - 1, 4, rows, width), F32),
        ),
        [(a, "v") for a in (own[-1], rest[0], own[3], rest[3], w, *arrays)],
        [pltpu.VMEM((4, rows, width), BF16)] * 2,
        min(60, 14 + 6 * layers),
    )


def dmix_of(dpre, w, k):
    beta = beta_of(k)
    return ((1.0 - beta) * dpre.astype(F32) + beta * mm_nt(dpre, w)).astype(BF16)


def back_start_call(cot, near, far, w, later_slope, matrix):
    arrays, readers = matrix
    layers = w.shape[0]
    rows, width = cot.shape
    piece = rows // layers
    m = len(arrays)
    last = layers - 1

    def body(cot_r, w_r, slope_r, *refs):
        own_at, near_at, far_at = readers(refs[:m])
        got_r = [refs[m + g * layers : m + (g + 1) * layers] for g in range(2)]
        dpre_o, sums_o, carry_o, up_s = refs[m + 2 * layers :]
        seg = lax.axis_index("segment")
        for g in range(2):
            for k in range(layers):
                up_s[g, piece_slice(seg, k, layers, piece), :] = got_r[g][k][...]
        dmix = []
        for g in range(3):
            up = up_s[g - 1] if g else cot_r[...]
            dpre = ((0.5 * up).astype(F32) * slope_r[last - 1, g]).astype(BF16)
            dpre_o[pl.ds(g * rows, rows), :] = dpre
            dmix.append(dmix_of(dpre, w_r[last], last))
        carry_o[...] = SHARE * dmix[0].astype(F32)
        sums_o[0] = mm_tn(along(0, own_at(0), near_at(1), far_at(2)), along(0, *dmix))
        sums_o[1] = mm_tn(along(0, near_at(0), own_at(1)), along(0, dmix[0], dmix[1]))
        sums_o[2] = mm_tn(along(0, far_at(0), own_at(2)), along(0, dmix[0], dmix[2]))
        sums_o[3] = mm_tn(along(0, far_at(1), near_at(2)), along(0, dmix[1], dmix[2]))

    return call(
        body,
        (sds((3 * rows, width), BF16), sds((4, rows, width), F32), sds((rows, width), F32)),
        [(a, "v") for a in (cot, w, later_slope, *arrays, *near, *far)],
        [pltpu.VMEM((2, rows, width), BF16)],
        min(60, 14 + 6 * layers),
    )


def back_call(diag, start, w, own, rest, later_mix, later_slope, matrix):
    arrays, readers = matrix
    dpre_start, sums, carry = start
    mix, slope = own[1], own[2]
    mix_rest, slope_rest = rest[1], rest[2]
    layers = w.shape[0]
    rows, width = mix.shape
    piece = rows // layers
    n_dom = lax.axis_size("dom")
    others = n_dom // 4
    out_rows = width // n_dom
    half = width // 2
    m = len(arrays)
    last = layers - 1

    def body(dps_r, sums_r, carry_r, mix_r, slope_r, mixn_r, slopen_r, later_mix_r, later_slope_r, w_r, *refs):
        own_at, near_at, far_at = readers(refs[:m])
        got_r = refs[m : m + layers]
        outs = refs[m + layers :]
        dpre_o, carry_o, mine_o = outs[:3]
        send_o = outs[3 : 2 + others]
        up_s, dmix_s, part_s = outs[2 + others :]
        seg, low, high, place = position()
        for k in range(layers):
            up_s[3, piece_slice(seg, k, layers, piece), :] = got_r[k][...]

        def weight_part(k, dpre_at):
            at = pl.ds(pl.multiple_of(high * half, half), half)
            chosen = [later_mix_r[k - 1, g, :, at] if k else (mixn_r[g - 1, :, at] if g else mix_r[:, at]) for g in range(4)]
            part_s[...] = beta_of(k) * mm_tn(along(0, *chosen), along(0, *[dpre_at(g) for g in range(4)]))

        dpre = ((0.5 * up_s[3]).astype(F32) * later_slope_r[last - 1, 3]).astype(BF16)
        dpre_o[pl.ds(3 * rows, rows), :] = dpre
        dmix = dmix_of(dpre, w_r[last], last)
        extra = (None, mm_tn(far_at(3), dmix), mm_tn(near_at(3), dmix), mm_tn(own_at(3), dmix))
        for g in range(4):
            total = sums_r[g] if g == 0 else sums_r[g] + extra[g]
            up_s[g] = ((0.5 - 0.5 * SHARE) * total).astype(BF16)

        @pl.when(seg == last)
        def _():
            weight_part(last, lambda g: dps_r[pl.ds(g * rows, rows), :] if g < 3 else dpre_o[pl.ds(g * rows, rows), :])

        carry_o[...] = carry_r[...]
        for k in range(last - 1, -1, -1):
            for g in range(4):
                slope_now = later_slope_r[k - 1, g] if k else (slopen_r[g - 1] if g else slope_r[...])
                dpre = (up_s[g].astype(F32) * slope_now).astype(BF16)
                dpre_o[pl.ds(g * rows, rows), :] = dpre
                if k:
                    dmix = dmix_of(dpre, w_r[k], k)
                    dmix_s[g] = dmix
                    if g == 0:
                        carry_o[...] = SHARE * dmix.astype(F32) + carry_o[...]

            @pl.when(seg == k)
            def _():
                weight_part(k, lambda g: dpre_o[pl.ds(g * rows, rows), :])

            if k:
                for g in range(4):
                    total = mm_tn(
                        along(0, own_at(g), near_at(g ^ 1), far_at(g ^ 2)), along(0, dmix_s[g], dmix_s[g ^ 1], dmix_s[g ^ 2])
                    )
                    up_s[g] = ((0.5 - 0.5 * SHARE) * total).astype(BF16)

        def block(b):
            at = (place ^ b) * (2 * out_rows) + low * out_rows
            return part_s[pl.ds(pl.multiple_of(at, out_rows), out_rows), :]

        mine_o[...] = block(0)
        for b in range(1, others):
            send_o[b - 1][...] = block(b).astype(BF16)

    got = call(
        body,
        (sds((4 * rows, width), BF16), sds((rows, width), F32), sds((out_rows, width), F32))
        + tuple(sds((out_rows, width), BF16) for _ in range(1, others)),
        [
            (a, "v")
            for a in (
                dpre_start,
                sums,
                carry,
                mix,
                slope,
                mix_rest,
                slope_rest,
                later_mix,
                later_slope,
                w,
                *arrays,
                *diag,
            )
        ],
        [
            pltpu.VMEM((4, rows, width), BF16),
            pltpu.VMEM((4, rows, width), BF16),
            pltpu.VMEM((half, width), F32),
        ],
        min(60, 14 + 6 * layers),
    )
    return got[0], got[1], got[2], got[3:]


def feat_call(dpre, carry, w, matrix):
    arrays, readers = matrix
    layers = w.shape[0]
    rows, width = carry.shape
    cols = width // layers
    sliced = cols % 128 == 0
    kept = cols if sliced else width
    m = len(arrays)
    beta = beta_of(0)

    def body(dpre_r, carry_r, w_r, *refs):
        own_at, near_at, far_at = readers(refs[:m])
        feat_o = refs[m]
        at = pl.ds(pl.multiple_of(lax.axis_index("segment") * cols, cols), cols) if sliced else slice(None)
        w_rows = w_r[0, at, :]
        dmix = []
        for g in range(3):
            d_at = pl.ds(g * rows, rows)
            through = mm_nt(dpre_r[d_at, :], w_rows)
            dmix.append(((1.0 - beta) * dpre_r[d_at, at].astype(F32) + beta * through).astype(BF16))
        sums = mm_tn(along(0, own_at(0), near_at(1), far_at(2)), along(0, *dmix))
        feat_o[...] = (1.0 - SHARE) * sums + (carry_r[:, at] + SHARE * dmix[0].astype(F32))

    (feat,) = call(body, (sds((rows, kept), F32),), [(a, "v") for a in (dpre, carry, w, *arrays)], vmem=12)
    return feat if sliced else lax.dynamic_slice_in_dim(feat, lax.axis_index("segment") * cols, cols, 1)


def step(feats, adj, couple, send_rows, weights, cot):
    layers = lax.axis_size("segment")
    n_dom = lax.axis_size("dom")
    top = n_dom // 2
    others = n_dom // 4

    fwd_mine, cot_mine = pack_call(feats, adj, couple, send_rows, cot, layers)
    far = swapped(fwd_mine, top)
    near = swapped(fwd_mine, 1)
    w_pieces = every_piece(weights)
    prep = prep_call(feats, adj, couple, send_rows)
    nears = every_piece(near)
    diag = swapped(far, 1)
    fars = every_piece(far)
    far_cot = swapped(cot_mine, top)
    own = own_call(nears, fars, w_pieces, prep)
    diags = every_piece(diag)
    near_cot = swapped(cot_mine, 1)
    rest = rest_call(diags, own)
    diag_cot = swapped(far_cot, 1)
    far_cots = every_piece(far_cot)
    near_cots = every_piece(near_cot)
    matrix = matrix_of(prep, own, rest)
    w = own[-2]
    acts, later_mix, later_slope = later_call(w, own, rest, matrix)
    diag_cots = every_piece(diag_cot)
    start = back_start_call(cot, near_cots, far_cots, w, later_slope, matrix)
    dpre, carry, wgrad, sends = back_call(diag_cots, start, w, own, rest, later_mix, later_slope, matrix
    )
    for m in range(1, others):
        wgrad = wgrad + swapped(sends[m - 1], 2 * m).astype(F32)
    feat = feat_call(dpre, carry, w, matrix)
    return (acts[None], wgrad[None], feat)


def solution(mesh):
    in_specs = (
        P("dom", None),
        P("dom", None),
        P("dom", None),
        P("dom", None),
        P("segment", None),
        P("dom", None),
    )
    out_specs = (P("segment", "dom", None), P("segment", "dom", None), P("dom", "segment"))
    return jax.shard_map(step, mesh=mesh, in_specs=in_specs, out_specs=out_specs, check_vma=False)
```

profile of v0, /device:TPU:0, one launch (start us, length us, event | category | flops | bytes accessed | tf_op | source)
XLA Modules:
  0.0 56.8 jit_solution(7324058993657695406)
XLA Ops:
  0.6 1.1 %shard_map.86 = (bf16[264,512]{1,0:T(8,128)(2,1)S(1)}, bf16[128,512]{1,0:T(8,128)(2,1)S(1)}) custom-call(bf16[256,512]{1,0:T(8,128)(2,1)} %feats_r.3, bf16[256,256]{1,0:T(8,128)(2,1)} %adj_r.3, bf16[256,256]{1,0:T(8,128)(2,1)} %couple_r.3, s32[1,256]{1,0:T(1,128)} %sr_r.3, bf16[256,512]{1,0:T(8,128)(2,1)} %cot_r.3), custom_call_target="tpu_custom_call" | custom-call | tf_op jit(solution)/shard_map/pallas_call | solution.py:60
  1.7 4.1 %collective-permute-start.2 = (bf16[264,512]{1,0:T(8,128)(2,1)S(1)}, bf16[264,512]{1,0:T(8,128)(2,1)S(1)}, u32[]{:S(2)}, u32[]{:S(2)}) collective-permute-start(bf16[264,512]{1,0:T(8,128)(2,1)S(1)} %get-tuple-element.45), channel_id=1, source_target_pairs={{0,16},{2,18},{4,20},{6,22},{8,24},{10,26},{12,28},{14,30},{16,0},... | collective-permute-start | bytes 811016 | tf_op jit(solution)/shard_map/ppermute | solution.py:18
  5.9 1.5 %collective-permute-start = (bf16[264,512]{1,0:T(8,128)(2,1)S(1)}, bf16[264,512]{1,0:T(8,128)(2,1)S(1)}, u32[]{:S(2)}, u32[]{:S(2)}) collective-permute-start(bf16[264,512]{1,0:T(8,128)(2,1)S(1)} %get-tuple-element.45), channel_id=1, source_target_pairs={{0,2},{2,0},{4,6},{6,4},{8,10},{10,8},{12,14},{14,12},{16,18},{18,... | collective-permute-start | bytes 811016 | tf_op jit(solution)/shard_map/ppermute | solution.py:18
  7.4 10.8 %collective-permute-done.2.refs_2_ = bf16[264,512]{1,0:T(8,128)(2,1)S(1)} collective-permute-done((bf16[264,512]{1,0:T(8,128)(2,1)S(1)}, bf16[264,512]{1,0:T(8,128)(2,1)S(1)}, u32[]{:S(2)}, u32[]{:S(2)}) %collective-permute-start.2) | collective-permute-done | bytes 270368 | tf_op jit(solution)/shard_map/ppermute | solution.py:18
  18.1 1.5 %collective-permute-start.5 = (bf16[264,512]{1,0:T(8,128)(2,1)S(1)}, bf16[264,512]{1,0:T(8,128)(2,1)S(1)}, u32[]{:S(2)}, u32[]{:S(2)}) collective-permute-start(bf16[264,512]{1,0:T(8,128)(2,1)S(1)} %collective-permute-done.2.refs_2_), channel_id=1, source_target_pairs={{0,2},{2,0},{4,6},{6,4},{8,10},{10,8},{12,14},{14,12},{16,18},{18,... | collective-permute-start | bytes 811016 | tf_op jit(solution)/shard_map/ppermute | solution.py:18
  19.7 0.0 collective-permute-start.9
  19.7 0.0 collective-permute-start.3
  19.7 8.3 %collective-permute-done.9.refs_9_ = bf16[128,512]{1,0:T(8,128)(2,1)S(1)} collective-permute-done((bf16[128,512]{1,0:T(8,128)(2,1)S(1)}, bf16[128,512]{1,0:T(8,128)(2,1)S(1)}, u32[]{:S(2)}, u32[]{:S(2)}) %collective-permute-start.9) | collective-permute-done | bytes 131104 | tf_op jit(solution)/shard_map/ppermute | solution.py:18
  28.0 0.5 collective-permute-start.7
  28.5 0.0 collective-permute-start.1
  28.5 0.0 collective-permute-done.5.refs_0_
  28.5 0.5 collective-permute-start.6
  29.0 5.2 %collective-permute-done.7.refs_7_ = bf16[128,512]{1,0:T(8,128)(2,1)S(1)} collective-permute-done((bf16[128,512]{1,0:T(8,128)(2,1)S(1)}, bf16[128,512]{1,0:T(8,128)(2,1)S(1)}, u32[]{:S(2)}, u32[]{:S(2)}) %collective-permute-start.7) | collective-permute-done | bytes 131104 | tf_op jit(solution)/shard_map/ppermute | solution.py:18
  34.2 5.0 %collective-permute-done.11.refs_7_ = bf16[128,512]{1,0:T(8,128)(2,1)S(1)} collective-permute-done((bf16[128,512]{1,0:T(8,128)(2,1)S(1)}, bf16[128,512]{1,0:T(8,128)(2,1)S(1)}, u32[]{:S(2)}, u32[]{:S(2)}) %collective-permute-start.11) | collective-permute-done | bytes 131104 | tf_op jit(solution)/shard_map/ppermute | solution.py:18
  39.2 0.5 collective-permute-start.8
  39.7 0.1 collective-permute-start.12
  39.7 1.3 %shard_map.85 = (bf16[256,512]{1,0:T(8,128)(2,1)S(1)}, bf16[256,256]{1,0:T(8,128)(2,1)S(1)}, bf16[256,256]{1,0:T(8,128)(2,1)S(1)}, bf16[256,256]{1,0:T(8,128)(2,1)S(1)}, f32[256,512]{1,0:T(8,128)S(1)}) custom-call(bf16[256,512]{1,0:T(8,128)(2,1)} %feats_r.3, bf16[256,256]{1,0:T(8,128)(2,1)} %adj_r.3, bf16[256,256]{1,0:T(8,128)(2,1)} %couple_r.3, s32[1,256]{1,0:T(1,128)} %sr_r.3), custom_call_target="tpu_custom_call" | custom-call | tf_op jit(solution)/shard_map/pallas_call | solution.py:60
  41.1 1.9 %shard_map.87 = (bf16[2,256,512]{2,1,0:T(8,128)(2,1)S(1)}, bf16[256,512]{1,0:T(8,128)(2,1)S(1)}, f32[256,512]{1,0:T(8,128)S(1)}, bf16[256,512]{1,0:T(8,128)(2,1)...) custom-call(bf16[256,512]{1,0:T(8,128)(2,1)S(1)} %get-tuple-element., ...), custom_call_target="tpu_custom_call" | custom-call | tf_op jit(solution)/shard_map/pallas_call | solution.py:60
  43.0 1.6 %shard_map.88 = (f32[256,512]{1,0:T(8,128)S(1)}, bf16[3,256,512]{2,1,0:T(8,128)(2,1)S(1)}, f32[3,256,512]{2,1,0:T(8,128)S(1)}, bf16[3,256,512]{2,1,0:T(8,128)(2,...) custom-call(bf16[2,256,512]{2,1,0:T(8,128)(2,1)S(1)} %get-tuple-element.47., ...), custom_call_target="tpu_custom_call" | custom-call | tf_op jit(solution)/shard_map/pallas_call | solution.py:60
  44.6 0.0 copy-start
  44.6 2.3 %shard_map.89 = (bf16[256,512]{1,0:T(8,128)(2,1)}, bf16[1,4,256,512]{3,2,1,0:T(8,128)(2,1)S(1)}, f32[1,4,256,512]{3,2,1,0:T(8,128)S(1)}) custom-call(f32[3,256,512]{2,1,0:T(8,128)S(1)} %get-tuple-element.46.first_r, f32[256,512]{1,0:T(8,128)S(1)} %get-tuple-element.52.first3_r, bf16[256,512]{1,0:T(8,128)(2,1)S(1)} %get-tuple-element.53.x1_r, ...), custom_call_target="tpu_custom_call" | custom-call | tf_op jit(solution)/shard_map/pallas_call | solution.py:60
  46.9 0.0 collective-permute-done.10.refs_10_
  46.9 1.4 %shard_map.90 = (bf16[768,512]{1,0:T(8,128)(2,1)S(1)}, f32[4,256,512]{2,1,0:T(8,128)S(1)}, f32[256,512]{1,0:T(8,128)S(1)}) custom-call(bf16[256,512]{1,0:T(8,128)(2,1)S(1)} %copy-done, bf16[2,512,512]{2,1,0:T(8,128)(2,1)S(1)} %get-tuple-element.51.w_r, f32[1,4,256,512]{3,2,1,0:T(8,128)S(1)} %get-tuple-element.63.slope_r.later_slope_r, ...), custom_call_target="tpu_custom_call" | custom-call | tf_op jit(solution)/shard_map/pallas_call | solution.py:60
  48.3 0.0 collective-permute-done.12.refs_8_
  48.3 1.4 %shard_map.91 = (bf16[1024,512]{1,0:T(8,128)(2,1)S(1)}, f32[256,512]{1,0:T(8,128)S(1)}, f32[32,512]{1,0:T(8,128)S(1)}, bf16[32,512]{1,0:T(8,128)(2,1)S(1)}, bf16...) custom-call(bf16[768,512]{1,0:T(8,128)(2,1)S(1)} %get-tuple-element.65.dps_r, ...), custom_call_target="tpu_custom_call" | custom-call | tf_op jit(solution)/shard_map/pallas_call | solution.py:60
  49.7 1.6 %collective-permute-start.13 = (bf16[32,512]{1,0:T(8,128)(2,1)S(1)}, bf16[32,512]{1,0:T(8,128)(2,1)S(1)}, u32[]{:S(2)}, u32[]{:S(2)}) collective-permute-start(bf16[32,512]{1,0:T(8,128)(2,1)S(1)} %get-tuple-element.74), channel_id=1, source_target_pairs={{0,4},{2,6},{4,0},{6,2},{8,12},{10,14},{12,8},{14,10},{16,20},{18,... | collective-permute-start | bytes 98312 | tf_op jit(solution)/shard_map/ppermute | solution.py:18
  51.3 0.0 collective-permute-start.14
  51.3 2.0 %collective-permute-start.15 = (bf16[32,512]{1,0:T(8,128)(2,1)S(1)}, bf16[32,512]{1,0:T(8,128)(2,1)S(1)}, u32[]{:S(2)}, u32[]{:S(2)}) collective-permute-start(bf16[32,512]{1,0:T(8,128)(2,1)S(1)} %get-tuple-element.76), channel_id=1, source_target_pairs={{0,12},{2,14},{4,8},{6,10},{8,4},{10,6},{12,0},{14,2},{16,28},{18,... | collective-permute-start | bytes 98312 | tf_op jit(solution)/shard_map/ppermute | solution.py:18
  53.3 1.4 %shard_map.92 = f32[256,256]{1,0:T(8,128)} custom-call(bf16[1024,512]{1,0:T(8,128)(2,1)S(1)} %get-tuple-element.77.dpre_r, f32[256,512]{1,0:T(8,128)S(1)} %get-tuple-element.78.carry_r, bf16[2,512,512]{2,1,0:T(8,128)(2,1)S(1)} %get-tuple-element.51.w_r, bf16[256,256]{1,0:T(8,128)(2,1)S(1)} %get-tuple-element.55.refs_0_, ...), custom_call_target="tpu_custom_call" | custom-call | tf_op jit(solution)/shard_map/pallas_call | solution.py:60
  54.7 0.6 %collective-permute-done.14 = bf16[32,512]{1,0:T(8,128)(2,1)S(1)} collective-permute-done((bf16[32,512]{1,0:T(8,128)(2,1)S(1)}, bf16[32,512]{1,0:T(8,128)(2,1)S(1)}, u32[]{:S(2)}, u32[]{:S(2)}) %collective-permute-start.14) | collective-permute-done | bytes 32800 | tf_op jit(solution)/shard_map/ppermute | solution.py:18
  55.2 0.9 %collective-permute-done.15 = bf16[32,512]{1,0:T(8,128)(2,1)S(1)} collective-permute-done((bf16[32,512]{1,0:T(8,128)(2,1)S(1)}, bf16[32,512]{1,0:T(8,128)(2,1)S(1)}, u32[]{:S(2)}, u32[]{:S(2)}) %collective-permute-start.15) | collective-permute-done | bytes 32800 | tf_op jit(solution)/shard_map/ppermute | solution.py:18
  56.1 0.6 %add_bitcast_fusion = f32[1,32,512]{2,1,0:T(8,128)} fusion(bf16[32,512]{1,0:T(8,128)(2,1)S(1)} %collective-permute-done.15, bf16[32,512]{1,0:T(8,128)(2,1)S(1)} %collective-permute-done.14, f32[32,512]{1,0:T(8,128)S(1)} %get-tuple-element.73, bf16[32,512]{1,0:T(8,128)(2,1)S(1)} %collective-permute-done.13), kind=kLoop, calls=%fused_computation | loop fusion | flops 98304 | bytes 229376 | tf_op jit(solution)/shard_map/broadcast_in_dim | solution.py:552
  (11 shorter events, 0.0 us)
Async XLA Ops:
  1.7 16.4 %collective-permute-start.2 = (bf16[264,512]{1,0:T(8,128)(2,1)S(1)}, bf16[264,512]{1,0:T(8,128)(2,1)S(1)}, u32[]{:S(2)}, u32[]{:S(2)}) collective-permute-start(bf16[264,512]{1,0:T(8,128)(2,1)S(1)} %get-tuple-element.45), channel_id=1, source_target_pairs={{0,16},{2,18},{4,20},{6,22},{8,24},{10,26},{12,28},{14,30},{16,0},... | collective-permute-start | bytes 811016 | tf_op jit(solution)/shard_map/ppermute | solution.py:18
  5.9 33.3 %collective-permute-start.4 = (bf16[512,512]{1,0:T(8,128)(2,1)}, bf16[512,512]{1,0:T(8,128)(2,1)S(1)}, u32[]{:S(2)}, u32[]{:S(2)}) collective-permute-start(bf16[512,512]{1,0:T(8,128)(2,1)} %refs_4_.1), channel_id=1, source_target_pairs={{0,1},{1,0},{2,3},{3,2},{4,5},{5,4},{6,7},{7,6},{8,9},{9,8},{10,11... | collective-permute-start | bytes 1572872 | tf_op jit(solution)/shard_map/ppermute | solution.py:23
  5.9 22.6 %collective-permute-start = (bf16[264,512]{1,0:T(8,128)(2,1)S(1)}, bf16[264,512]{1,0:T(8,128)(2,1)S(1)}, u32[]{:S(2)}, u32[]{:S(2)}) collective-permute-start(bf16[264,512]{1,0:T(8,128)(2,1)S(1)} %get-tuple-element.45), channel_id=1, source_target_pairs={{0,2},{2,0},{4,6},{6,4},{8,10},{10,8},{12,14},{14,12},{16,18},{18,... | collective-permute-start | bytes 811016 | tf_op jit(solution)/shard_map/ppermute | solution.py:18
  18.1 10.4 %collective-permute-start.5 = (bf16[264,512]{1,0:T(8,128)(2,1)S(1)}, bf16[264,512]{1,0:T(8,128)(2,1)S(1)}, u32[]{:S(2)}, u32[]{:S(2)}) collective-permute-start(bf16[264,512]{1,0:T(8,128)(2,1)S(1)} %collective-permute-done.2.refs_2_), channel_id=1, source_target_pairs={{0,2},{2,0},{4,6},{6,4},{8,10},{10,8},{12,14},{14,12},{16,18},{18,... | collective-permute-start | bytes 811016 | tf_op jit(solution)/shard_map/ppermute | solution.py:18
  19.7 8.3 %collective-permute-start.9 = (bf16[128,512]{1,0:T(8,128)(2,1)S(1)}, bf16[128,512]{1,0:T(8,128)(2,1)S(1)}, u32[]{:S(2)}, u32[]{:S(2)}) collective-permute-start(bf16[128,512]{1,0:T(8,128)(2,1)S(1)} %get-tuple-element.64), channel_id=1, source_target_pairs={{0,16},{2,18},{4,20},{6,22},{8,24},{10,26},{12,28},{14,30},{16,0},... | collective-permute-start | bytes 393224 | tf_op jit(solution)/shard_map/ppermute | solution.py:18
  19.7 20.0 %collective-permute-start.3 = (bf16[264,512]{1,0:T(8,128)(2,1)S(1)}, bf16[264,512]{1,0:T(8,128)(2,1)S(1)}, u32[]{:S(2)}, u32[]{:S(2)}) collective-permute-start(bf16[264,512]{1,0:T(8,128)(2,1)S(1)} %collective-permute-done.2.refs_2_), channel_id=1, source_target_pairs={{0,1},{1,0},{2,3},{3,2},{4,5},{5,4},{6,7},{7,6},{8,9},{9,8},{10,11... | collective-permute-start | bytes 811016 | tf_op jit(solution)/shard_map/ppermute | solution.py:23
  28.0 6.2 %collective-permute-start.7 = (bf16[128,512]{1,0:T(8,128)(2,1)S(1)}, bf16[128,512]{1,0:T(8,128)(2,1)S(1)}, u32[]{:S(2)}, u32[]{:S(2)}) collective-permute-start(bf16[128,512]{1,0:T(8,128)(2,1)S(1)} %get-tuple-element.64), channel_id=1, source_target_pairs={{0,2},{2,0},{4,6},{6,4},{8,10},{10,8},{12,14},{14,12},{16,18},{18,... | collective-permute-start | bytes 393224 | tf_op jit(solution)/shard_map/ppermute | solution.py:18
  28.5 12.6 %collective-permute-start.1 = (bf16[264,512]{1,0:T(8,128)(2,1)S(1)}, bf16[264,512]{1,0:T(8,128)(2,1)S(1)}, u32[]{:S(2)}, u32[]{:S(2)}) collective-permute-start(bf16[264,512]{1,0:T(8,128)(2,1)S(1)} %collective-permute-done.refs_0_), channel_id=1, source_target_pairs={{0,1},{1,0},{2,3},{3,2},{4,5},{5,4},{6,7},{7,6},{8,9},{9,8},{10,11... | collective-permute-start | bytes 811016 | tf_op jit(solution)/shard_map/ppermute | solution.py:23
  28.5 14.5 %collective-permute-start.6 = (bf16[264,512]{1,0:T(8,128)(2,1)S(1)}, bf16[264,512]{1,0:T(8,128)(2,1)S(1)}, u32[]{:S(2)}, u32[]{:S(2)}) collective-permute-start(bf16[264,512]{1,0:T(8,128)(2,1)S(1)} %collective-permute-done.5.refs_0_), channel_id=1, source_target_pairs={{0,1},{1,0},{2,3},{3,2},{4,5},{5,4},{6,7},{7,6},{8,9},{9,8},{10,11... | collective-permute-start | bytes 811016 | tf_op jit(solution)/shard_map/ppermute | solution.py:23
  34.2 5.0 %collective-permute-start.11 = (bf16[128,512]{1,0:T(8,128)(2,1)S(1)}, bf16[128,512]{1,0:T(8,128)(2,1)S(1)}, u32[]{:S(2)}, u32[]{:S(2)}) collective-permute-start(bf16[128,512]{1,0:T(8,128)(2,1)S(1)} %collective-permute-done.9.refs_9_), channel_id=1, source_target_pairs={{0,2},{2,0},{4,6},{6,4},{8,10},{10,8},{12,14},{14,12},{16,18},{18,... | collective-permute-start | bytes 393224 | tf_op jit(solution)/shard_map/ppermute | solution.py:18
  39.2 7.7 %collective-permute-start.10 = (bf16[128,512]{1,0:T(8,128)(2,1)S(1)}, bf16[128,512]{1,0:T(8,128)(2,1)S(1)}, u32[]{:S(2)}, u32[]{:S(2)}) collective-permute-start(bf16[128,512]{1,0:T(8,128)(2,1)S(1)} %collective-permute-done.9.refs_9_), channel_id=1, source_target_pairs={{0,1},{1,0},{2,3},{3,2},{4,5},{5,4},{6,7},{7,6},{8,9},{9,8},{10,11... | collective-permute-start | bytes 393224 | tf_op jit(solution)/shard_map/ppermute | solution.py:23
  39.2 7.7 %collective-permute-start.8 = (bf16[128,512]{1,0:T(8,128)(2,1)S(1)}, bf16[128,512]{1,0:T(8,128)(2,1)S(1)}, u32[]{:S(2)}, u32[]{:S(2)}) collective-permute-start(bf16[128,512]{1,0:T(8,128)(2,1)S(1)} %collective-permute-done.7.refs_7_), channel_id=1, source_target_pairs={{0,1},{1,0},{2,3},{3,2},{4,5},{5,4},{6,7},{7,6},{8,9},{9,8},{10,11... | collective-permute-start | bytes 393224 | tf_op jit(solution)/shard_map/ppermute | solution.py:23
  39.7 8.6 %collective-permute-start.12 = (bf16[128,512]{1,0:T(8,128)(2,1)S(1)}, bf16[128,512]{1,0:T(8,128)(2,1)S(1)}, u32[]{:S(2)}, u32[]{:S(2)}) collective-permute-start(bf16[128,512]{1,0:T(8,128)(2,1)S(1)} %collective-permute-done.11.refs_7_), channel_id=1, source_target_pairs={{0,1},{1,0},{2,3},{3,2},{4,5},{5,4},{6,7},{7,6},{8,9},{9,8},{10,11... | collective-permute-start | bytes 393224 | tf_op jit(solution)/shard_map/ppermute | solution.py:23
  44.6 2.3 %copy-start = (bf16[256,512]{1,0:T(8,128)(2,1)S(1)}, bf16[256,512]{1,0:T(8,128)(2,1)}, u32[]{:S(2)}) copy-start(bf16[256,512]{1,0:T(8,128)(2,1)} %cot_r.3) | copy-start | bytes 786436
  49.7 4.9 %collective-permute-start.13 = (bf16[32,512]{1,0:T(8,128)(2,1)S(1)}, bf16[32,512]{1,0:T(8,128)(2,1)S(1)}, u32[]{:S(2)}, u32[]{:S(2)}) collective-permute-start(bf16[32,512]{1,0:T(8,128)(2,1)S(1)} %get-tuple-element.74), channel_id=1, source_target_pairs={{0,4},{2,6},{4,0},{6,2},{8,12},{10,14},{12,8},{14,10},{16,20},{18,... | collective-permute-start | bytes 98312 | tf_op jit(solution)/shard_map/ppermute | solution.py:18
  51.3 3.9 %collective-permute-start.14 = (bf16[32,512]{1,0:T(8,128)(2,1)S(1)}, bf16[32,512]{1,0:T(8,128)(2,1)S(1)}, u32[]{:S(2)}, u32[]{:S(2)}) collective-permute-start(bf16[32,512]{1,0:T(8,128)(2,1)S(1)} %get-tuple-element.75), channel_id=1, source_target_pairs={{0,8},{2,10},{4,12},{6,14},{8,0},{10,2},{12,4},{14,6},{16,24},{18,... | collective-permute-start | bytes 98312 | tf_op jit(solution)/shard_map/ppermute | solution.py:18
  51.3 4.8 %collective-permute-start.15 = (bf16[32,512]{1,0:T(8,128)(2,1)S(1)}, bf16[32,512]{1,0:T(8,128)(2,1)S(1)}, u32[]{:S(2)}, u32[]{:S(2)}) collective-permute-start(bf16[32,512]{1,0:T(8,128)(2,1)S(1)} %get-tuple-element.76), channel_id=1, source_target_pairs={{0,12},{2,14},{4,8},{6,10},{8,4},{10,6},{12,0},{14,2},{16,28},{18,... | collective-permute-start | bytes 98312 | tf_op jit(solution)/shard_map/ppermute | solution.py:18
where the time goes:
time: 57 us; the launch traced here: 56.8 us
  waiting for transfers between devices  30.7 us (54%)
  Pallas kernels  12.3 us (22%)
  starting transfers between devices  12.3 us (22%)
  between operations  0.76 us (1%)
  other arithmetic  0.65 us (1%)
    ppermute x9, waiting for transfers between devices, swapped(): lax.ppermute(x, 'dom', [(i, i ^ mask) for i in range(lax.axis_size('dom'))])  30.7 us
    pallas_call x8, Pallas kernels, call(): pl.pallas_call(body, out_shape=tuple(out_shape), in_specs=specs, out_spec...  12.3 us
    ppermute x9, starting transfers between devices, swapped(): lax.ppermute(x, 'dom', [(i, i ^ mask) for i in range(lax.axis_size('dom'))])  11.3 us
  transfers between devices with their start and end apart: 16, of which 6 were waited for; matrix products, arithmetic and copies ran while one was open for 0% of the time, Pallas kernels for 17%

commit v1 on v0

--- a/solution.py
+++ b/solution.py
@@ -70,35 +70,29 @@
 sds = jax.ShapeDtypeStruct
 
 
-def pack_call(feats, adj, couple, send_rows, cot, layers):
+def pack_call(feats, adj, couple, cot, layers):
     rows, width = feats.shape
     piece = rows // layers
-    picked = send_rows.shape[1]
-
-    def body(feats_r, adj_r, couple_r, sr_r, cot_r, fwd_o, cot_o, sr_s, sems):
+
+    def body(feats_r, adj_r, couple_r, cot_r, fwd_o, cot_o, sems):
         at = pl.ds(pl.multiple_of(lax.axis_index("segment") * piece, piece), piece)
         split = adj_r.shape[1]
         copies = [
-            pltpu.make_async_copy(adj_r.at[at, :], fwd_o.at[:piece, :split], sems.at[1]),
-            pltpu.make_async_copy(couple_r.at[at, :], fwd_o.at[:piece, split:], sems.at[2]),
-            pltpu.make_async_copy(feats_r.at[at, :], fwd_o.at[piece : 2 * piece, :], sems.at[0]),
+            pltpu.make_async_copy(adj_r.at[at, :], fwd_o.at[:piece, :split], sems.at[0]),
+            pltpu.make_async_copy(couple_r.at[at, :], fwd_o.at[:piece, split:], sems.at[1]),
+            pltpu.make_async_copy(feats_r.at[at, :], fwd_o.at[piece:, :], sems.at[2]),
             pltpu.make_async_copy(cot_r.at[at, :], cot_o, sems.at[3]),
         ]
-        sr_copy = pltpu.make_async_copy(sr_r, sr_s, sems.at[4])
-        sr_copy.start()
         for c in copies:
             c.start()
-        fwd_o[2 * piece :, picked:] = jnp.zeros((8, width - picked), BF16)
-        sr_copy.wait()
-        fwd_o[2 * piece :, :picked] = jnp.broadcast_to(sr_s[...].astype(F32), (8, picked)).astype(BF16)
         for c in copies:
             c.wait()
 
     return call(
         body,
-        (sds((2 * piece + 8, width), BF16), sds((piece, width), BF16)),
-        [(feats, "h"), (adj, "h"), (couple, "h"), (send_rows, "h"), (cot, "h")],
-        [pltpu.VMEM(send_rows.shape, jnp.int32), pltpu.SemaphoreType.DMA((5,))],
+        (sds((2 * piece, width), BF16), sds((piece, width), BF16)),
+        [(feats, "h"), (adj, "h"), (couple, "h"), (cot, "h")],
+        [pltpu.SemaphoreType.DMA((4,))],
         4,
     )
 
@@ -116,9 +110,9 @@
     return ((1.0 - SHARE) * agg + first_scaled).astype(BF16)
 
 
-def activate(mixed, w, k):
+def activate(mixed, through, k):
     beta = beta_of(k)
-    half = (0.5 - 0.5 * beta) * mixed.astype(F32) + (0.5 * beta) * mm(mixed, w)
+    half = (0.5 - 0.5 * beta) * mixed.astype(F32) + (0.5 * beta) * through
     t = jnp.tanh(half)
     up = 1.0 + t
     return up * (1.0 + half * (1.0 - t)), (half * up).astype(BF16)
@@ -164,18 +158,18 @@
     )
 
 
-def own_call(near, far, w_pieces, prep):
+def own_call(near, far, near_sr, far_sr, w_pieces, prep):
     x, _, couple, pick, agg = prep
     layers = len(near)
     rows, width = x.shape
     piece = rows // layers
     bound = couple.shape[1] // 2
 
-    def body(x_r, couple_r, pick_r, agg_r, *refs):
+    def body(x_r, couple_r, pick_r, agg_r, near_sr_r, far_sr_r, *refs):
         got_r = [refs[g * layers : (g + 1) * layers] for g in range(2)]
         w_r = refs[2 * layers : 3 * layers]
         outs = refs[3 * layers :]
-        x12_o, mix_o, slope_o, x1_o, sums_o, own12_o, near01_o, far02_o, cp_o, pick_o, w_o, first_o, ac_s, sem = outs
+        x12_o, mix_o, slope_o, x1_o, sums_o, own12_o, near01_o, far02_o, cp_o, pick_o, w_o, first_o, wt_o, ac_s, sem = outs
         seg = lax.axis_index("segment")
         w_copy = pltpu.make_async_copy(w_r[0], w_o.at[seg], sem)
         w_copy.start()
@@ -188,7 +182,7 @@
                 own12_o[g, at, :] = got_r[g][k][:piece, :rows]
                 ac_s[g, at, :] = got_r[g][k][:piece, rows:]
                 x12_o[g, at, :] = got_r[g][k][piece : 2 * piece, :]
-            picks.append(picks_of(got_r[g][0][2 * piece : 2 * piece + 1, : 2 * bound].astype(F32), rows))
+            picks.append(picks_of((near_sr_r, far_sr_r)[g][...].astype(F32), rows))
         near01_o[0] = mm_nt(couple_r[:, :bound], picks[0][:, :bound]).astype(BF16)
         far02_o[0] = mm_nt(couple_r[:, bound:], picks[1][:, bound:]).astype(BF16)
         near01_o[1] = mm_nt(ac_s[0, :, :bound], pick_r[:, :bound]).astype(BF16)
@@ -203,10 +197,12 @@
         first_o[1] = scaled(x12_o[0])
         first_o[2] = scaled(x12_o[1])
         w_copy.wait()
+        for k in range(layers):
+            wt_o[k] = w_o[k].T
         agg = agg_r[...] + mm(along(1, near01_o[0], far02_o[0]), along(0, x12_o[0], x12_o[1]))
         mixed = mixed_of(agg, first_o[0])
         mix_o[...] = mixed
-        slope_o[...], x1_o[...] = activate(mixed, w_o[0], 0)
+        slope_o[...], x1_o[...] = activate(mixed, mm(mixed, w_o[0]), 0)
 
     return call(
         body,
@@ -223,8 +219,9 @@
             sds((2, rows, bound), BF16),
             sds((layers, width, width), BF16),
             sds((3, rows, width), F32),
+            sds((layers, width, width), BF16),
         ),
-        [(a, "v") for a in (x, couple, pick, agg, *near, *far)]
+        [(a, "v") for a in (x, couple, pick, agg, near_sr, far_sr, *near, *far)]
         + [(w_pieces[0], "h")]
         + [(w, "v") for w in w_pieces[1:]],
         [pltpu.VMEM((2, rows, 2 * bound), BF16), pltpu.SemaphoreType.DMA],
@@ -232,14 +229,14 @@
     )
 
 
-def rest_call(diag, own):
-    x12, _, _, _, sums, _, _, _, cp, pick, w, first = own
+def rest_call(diag, diag_sr, own):
+    x12, _, _, _, sums, _, _, _, cp, pick, w, first, _ = own
     layers = len(diag)
     _, rows, width = x12.shape
     piece = rows // layers
     bound = cp.shape[2]
 
-    def body(x12_r, sums_r, cp_r, pick_r, w_r, first_r, *refs):
+    def body(x12_r, sums_r, cp_r, pick_r, w_r, first_r, sr_r, *refs):
         got_r = refs[:layers]
         first3_o, x3_s, mix_o, slope_o, x1_o, own3_o, near23_o, far13_o, ac_s = (refs[layers], refs[-1], *refs[layers + 1 : -1])
         seg = lax.axis_index("segment")
@@ -249,7 +246,7 @@
             ac_s[at, :] = got_r[k][:piece, rows:]
             x3_s[at, :] = got_r[k][piece : 2 * piece, :]
         first3_o[...] = scaled(x3_s[...])
-        picks = picks_of(got_r[0][2 * piece : 2 * piece + 1, : 2 * bound].astype(F32), rows)
+        picks = picks_of(sr_r[...].astype(F32), rows)
         far13_o[0] = mm_nt(cp_r[0], picks[:, bound:]).astype(BF16)
         near23_o[0] = mm_nt(cp_r[1], picks[:, :bound]).astype(BF16)
         near23_o[1] = mm_nt(ac_s[:, :bound], pick_r[1]).astype(BF16)
@@ -261,7 +258,9 @@
                 agg = mm(along(1, own3_o[...], near23_o[1], far13_o[1]), along(0, x3_s[...], x12_r[1], x12_r[0]))
             mixed = mixed_of(agg, first_r[g + 1] if g < 2 else first3_o[...])
             mix_o[g] = mixed
-            slope_o[g], x1_o[g] = activate(mixed, w_r[0], 0)
+        through = mm(along(0, *[mix_o[g] for g in range(3)]), w_r[0])
+        for g in range(3):
+            slope_o[g], x1_o[g] = activate(mix_o[g], through[g * rows : (g + 1) * rows], 0)
 
     return call(
         body,
@@ -274,7 +273,7 @@
             sds((2, rows, rows), BF16),
             sds((2, rows, rows), BF16),
         ),
-        [(a, "v") for a in (x12, sums, cp, pick, w, first, *diag)],
+        [(a, "v") for a in (x12, sums, cp, pick, w, first, diag_sr, *diag)],
         [pltpu.VMEM((rows, 2 * bound), BF16), pltpu.VMEM((rows, width), BF16)],
         16,
     )
@@ -318,7 +317,9 @@
                 agg = mm(along(1, own_at(g), near_at(g), far_at(g)), along(0, src(g), src(g ^ 1), src(g ^ 2)))
                 mixed = mixed_of(agg, first_r[g] if g < 3 else first3_r[...])
                 mix_o[k - 1, g] = mixed
-                slope_o[k - 1, g], out = activate(mixed, w_r[k], k)
+            through = mm(along(0, *[mix_o[k - 1, g] for g in range(4)]), w_r[k])
+            for g in range(4):
+                slope_o[k - 1, g], out = activate(mix_o[k - 1, g], through[g * rows : (g + 1) * rows], k)
                 if k + 1 < layers:
                     dst[g] = out
                 if g == 0:
@@ -337,15 +338,15 @@
             sds((layers - 1, 4, rows, width), BF16),
             sds((layers - 1, 4, rows, width), F32),
         ),
-        [(a, "v") for a in (own[-1], rest[0], own[3], rest[3], w, *arrays)],
+        [(a, "v") for a in (own[-2], rest[0], own[3], rest[3], w, *arrays)],
         [pltpu.VMEM((4, rows, width), BF16)] * 2,
         min(60, 14 + 6 * layers),
     )
 
 
-def dmix_of(dpre, w, k):
+def dmix_of(dpre, w_t, k):
     beta = beta_of(k)
-    return ((1.0 - beta) * dpre.astype(F32) + beta * mm_nt(dpre, w)).astype(BF16)
+    return ((1.0 - beta) * dpre.astype(F32) + beta * mm(dpre, w_t)).astype(BF16)
 
 
 def back_start_call(cot, near, far, w, later_slope, matrix):
@@ -504,11 +505,11 @@
         own_at, near_at, far_at = readers(refs[:m])
         feat_o = refs[m]
         at = pl.ds(pl.multiple_of(lax.axis_index("segment") * cols, cols), cols) if sliced else slice(None)
-        w_rows = w_r[0, at, :]
+        w_cols = w_r[0, :, at]
         dmix = []
         for g in range(3):
             d_at = pl.ds(g * rows, rows)
-            through = mm_nt(dpre_r[d_at, :], w_rows)
+            through = mm(dpre_r[d_at, :], w_cols)
             dmix.append(((1.0 - beta) * dpre_r[d_at, at].astype(F32) + beta * through).astype(BF16))
         sums = mm_tn(along(0, own_at(0), near_at(1), far_at(2)), along(0, *dmix))
         feat_o[...] = (1.0 - SHARE) * sums + (carry_r[:, at] + SHARE * dmix[0].astype(F32))
@@ -523,32 +524,35 @@
     top = n_dom // 2
     others = n_dom // 4
 
-    fwd_mine, cot_mine = pack_call(feats, adj, couple, send_rows, cot, layers)
+    fwd_mine, cot_mine = pack_call(feats, adj, couple, cot, layers)
     far = swapped(fwd_mine, top)
     near = swapped(fwd_mine, 1)
     w_pieces = every_piece(weights)
+    far_sr = swapped(send_rows, top)
+    near_sr = swapped(send_rows, 1)
+    diag_sr = swapped(send_rows, top + 1)
     prep = prep_call(feats, adj, couple, send_rows)
     nears = every_piece(near)
     diag = swapped(far, 1)
     fars = every_piece(far)
     far_cot = swapped(cot_mine, top)
-    own = own_call(nears, fars, w_pieces, prep)
+    own = own_call(nears, fars, near_sr, far_sr, w_pieces, prep)
     diags = every_piece(diag)
     near_cot = swapped(cot_mine, 1)
-    rest = rest_call(diags, own)
+    rest = rest_call(diags, diag_sr, own)
     diag_cot = swapped(far_cot, 1)
     far_cots = every_piece(far_cot)
     near_cots = every_piece(near_cot)
     matrix = matrix_of(prep, own, rest)
-    w = own[-2]
+    w, w_t = own[-3], own[-1]
     acts, later_mix, later_slope = later_call(w, own, rest, matrix)
     diag_cots = every_piece(diag_cot)
-    start = back_start_call(cot, near_cots, far_cots, w, later_slope, matrix)
-    dpre, carry, wgrad, sends = back_call(diag_cots, start, w, own, rest, later_mix, later_slope, matrix
+    start = back_start_call(cot, near_cots, far_cots, w_t, later_slope, matrix)
+    dpre, carry, wgrad, sends = back_call(diag_cots, start, w_t, own, rest, later_mix, later_slope, matrix
     )
     for m in range(1, others):
         wgrad = wgrad + swapped(sends[m - 1], 2 * m).astype(F32)
-    feat = feat_call(dpre, carry, w, matrix)
+    feat = feat_call(dpre, carry, w_t, matrix)
     return (acts[None], wgrad[None], feat)
 
 

time: 57 us -> 64 us (1.12)
  starting transfers between devices: 12.3 us -> 19.1 us
    ppermute x9 -> x12, starting transfers between devices: 11.3 us -> 18 us  [swapped(): lax.ppermute(x, 'dom', [(i, i ^ mask) for i in range(lax.axis_size('dom'))])]
    ppermute x9 -> x12, waiting for transfers between devices: 30.7 us -> 31.1 us  [swapped(): lax.ppermute(x, 'dom', [(i, i ^ mask) for i in range(lax.axis_size('dom'))])]
  transfers between devices with their start and end apart: 16 -> 19, of which waited for: 6 -> 8; matrix products, arithmetic and copies ran while one was open for 0% -> 0% of each run, Pallas kernels for 17% -> 15%
where the time goes in v1:
time: 64 us; the launch traced here: 63.8 us
  waiting for transfers between devices  31.1 us (49%)
  starting transfers between devices  19.1 us (30%)
  Pallas kernels  12.2 us (19%)
  between operations  0.72 us (1%)
  other arithmetic  0.65 us (1%)
    ppermute x12, waiting for transfers between devices, swapped(): lax.ppermute(x, 'dom', [(i, i ^ mask) for i in range(lax.axis_size('dom'))])  31.1 us
    ppermute x12, starting transfers between devices, swapped(): lax.ppermute(x, 'dom', [(i, i ^ mask) for i in range(lax.axis_size('dom'))])  18 us
    pallas_call x8, Pallas kernels, call(): pl.pallas_call(body, out_shape=tuple(out_shape), in_specs=specs, out_spec...  12.2 us
  transfers between devices with their start and end apart: 19, of which 8 were waited for; matrix products, arithmetic and copies ran while one was open for 0% of the time, Pallas kernels for 15%

profile of v1, /device:TPU:0, one launch (start us, length us, event | category | flops | bytes accessed | tf_op | source)
XLA Modules:
  0.0 63.8 jit_solution(7739737714951602884)
XLA Ops:
  0.6 1.1 %shard_map.86 = (bf16[256,512]{1,0:T(8,128)(2,1)S(1)}, bf16[128,512]{1,0:T(8,128)(2,1)S(1)}) custom-call(bf16[256,512]{1,0:T(8,128)(2,1)} %feats_r.3, bf16[256,256]{1,0:T(8,128)(2,1)} %adj_r.3, bf16[256,256]{1,0:T(8,128)(2,1)} %couple_r.3, bf16[256,512]{1,0:T(8,128)(2,1)} %cot_r.3), custom_call_target="tpu_custom_call" | custom-call | tf_op jit(solution)/shard_map/pallas_call | solution.py:60
  1.7 4.1 %collective-permute-start.4 = (bf16[256,512]{1,0:T(8,128)(2,1)S(1)}, bf16[256,512]{1,0:T(8,128)(2,1)S(1)}, u32[]{:S(2)}, u32[]{:S(2)}) collective-permute-start(bf16[256,512]{1,0:T(8,128)(2,1)S(1)} %get-tuple-element.46), channel_id=1, source_target_pairs={{0,16},{2,18},{4,20},{6,22},{8,24},{10,26},{12,28},{14,30},{16,0},... | collective-permute-start | bytes 786440 | tf_op jit(solution)/shard_map/ppermute | solution.py:18
  5.9 1.5 %collective-permute-start.2 = (bf16[256,512]{1,0:T(8,128)(2,1)S(1)}, bf16[256,512]{1,0:T(8,128)(2,1)S(1)}, u32[]{:S(2)}, u32[]{:S(2)}) collective-permute-start(bf16[256,512]{1,0:T(8,128)(2,1)S(1)} %get-tuple-element.46), channel_id=1, source_target_pairs={{0,2},{2,0},{4,6},{6,4},{8,10},{10,8},{12,14},{14,12},{16,18},{18,... | collective-permute-start | bytes 786440 | tf_op jit(solution)/shard_map/ppermute | solution.py:18
  7.3 10.4 %collective-permute-done.4.refs_2_ = bf16[256,512]{1,0:T(8,128)(2,1)S(1)} collective-permute-done((bf16[256,512]{1,0:T(8,128)(2,1)S(1)}, bf16[256,512]{1,0:T(8,128)(2,1)S(1)}, u32[]{:S(2)}, u32[]{:S(2)}) %collective-permute-start.4) | collective-permute-done | bytes 262176 | tf_op jit(solution)/shard_map/ppermute | solution.py:18
  17.8 1.5 %collective-permute-start.8 = (bf16[256,512]{1,0:T(8,128)(2,1)S(1)}, bf16[256,512]{1,0:T(8,128)(2,1)S(1)}, u32[]{:S(2)}, u32[]{:S(2)}) collective-permute-start(bf16[256,512]{1,0:T(8,128)(2,1)S(1)} %collective-permute-done.4.refs_2_), channel_id=1, source_target_pairs={{0,2},{2,0},{4,6},{6,4},{8,10},{10,8},{12,14},{14,12},{16,18},{18,... | collective-permute-start | bytes 786440 | tf_op jit(solution)/shard_map/ppermute | solution.py:18
  19.3 0.5 collective-permute-start
  19.8 5.5 %collective-permute-done.near_sr_r = s32[1,256]{1,0:T(1,128)S(1)} collective-permute-done((s32[1,256]{1,0:T(1,128)}, s32[1,256]{1,0:T(1,128)S(1)}, u32[]{:S(2)}, u32[]{:S(2)}) %collective-permute-start) | collective-permute-done | bytes 1056 | tf_op jit(solution)/shard_map/ppermute | solution.py:18
  25.3 0.7 %collective-permute-start.1 = (s32[1,256]{1,0:T(1,128)}, s32[1,256]{1,0:T(1,128)S(1)}, u32[]{:S(2)}, u32[]{:S(2)}) collective-permute-start(s32[1,256]{1,0:T(1,128)} %sr_r.1), channel_id=1, source_target_pairs={{0,16},{2,18},{4,20},{6,22},{8,24},{10,26},{12,28},{14,30},{16,0},... | collective-permute-start | bytes 3080 | tf_op jit(solution)/shard_map/ppermute | solution.py:18
  26.0 4.0 %collective-permute-done.1.far_sr_r = s32[1,256]{1,0:T(1,128)S(1)} collective-permute-done((s32[1,256]{1,0:T(1,128)}, s32[1,256]{1,0:T(1,128)S(1)}, u32[]{:S(2)}, u32[]{:S(2)}) %collective-permute-start.1) | collective-permute-done | bytes 1056 | tf_op jit(solution)/shard_map/ppermute | solution.py:18
  30.0 1.3 %collective-permute-start.10 = (bf16[128,512]{1,0:T(8,128)(2,1)S(1)}, bf16[128,512]{1,0:T(8,128)(2,1)S(1)}, u32[]{:S(2)}, u32[]{:S(2)}) collective-permute-start(bf16[128,512]{1,0:T(8,128)(2,1)S(1)} %get-tuple-element.66), channel_id=1, source_target_pairs={{0,2},{2,0},{4,6},{6,4},{8,10},{10,8},{12,14},{14,12},{16,18},{18,... | collective-permute-start | bytes 393224 | tf_op jit(solution)/shard_map/ppermute | solution.py:18
  31.3 0.5 collective-permute-start.3
  31.8 0.1 collective-permute-start.9
  31.9 3.1 %collective-permute-done.10.refs_7_ = bf16[128,512]{1,0:T(8,128)(2,1)S(1)} collective-permute-done((bf16[128,512]{1,0:T(8,128)(2,1)S(1)}, bf16[128,512]{1,0:T(8,128)(2,1)S(1)}, u32[]{:S(2)}, u32[]{:S(2)}) %collective-permute-start.10) | collective-permute-done | bytes 131104 | tf_op jit(solution)/shard_map/ppermute | solution.py:18
  35.0 1.8 %collective-permute-start.14 = (bf16[128,512]{1,0:T(8,128)(2,1)S(1)}, bf16[128,512]{1,0:T(8,128)(2,1)S(1)}, u32[]{:S(2)}, u32[]{:S(2)}) collective-permute-start(bf16[128,512]{1,0:T(8,128)(2,1)S(1)} %collective-permute-done.12.refs_9_), channel_id=1, source_target_pairs={{0,2},{2,0},{4,6},{6,4},{8,10},{10,8},{12,14},{14,12},{16,18},{18,... | collective-permute-start | bytes 393224 | tf_op jit(solution)/shard_map/ppermute | solution.py:18
  36.8 3.1 %collective-permute-done.14.refs_7_ = bf16[128,512]{1,0:T(8,128)(2,1)S(1)} collective-permute-done((bf16[128,512]{1,0:T(8,128)(2,1)S(1)}, bf16[128,512]{1,0:T(8,128)(2,1)S(1)}, u32[]{:S(2)}, u32[]{:S(2)}) %collective-permute-start.14) | collective-permute-done | bytes 131104 | tf_op jit(solution)/shard_map/ppermute | solution.py:18
  40.0 0.5 collective-permute-start.11
  40.5 0.1 collective-permute-start.15
  40.6 0.9 %collective-permute-start.7 = (s32[1,256]{1,0:T(1,128)}, s32[1,256]{1,0:T(1,128)S(1)}, u32[]{:S(2)}, u32[]{:S(2)}) collective-permute-start(s32[1,256]{1,0:T(1,128)} %sr_r.1), channel_id=1, source_target_pairs={{0,18},{2,16},{4,22},{6,20},{8,26},{10,24},{12,30},{14,28},{16,2},... | collective-permute-start | bytes 3080 | tf_op jit(solution)/shard_map/ppermute | solution.py:18
  41.4 1.3 %shard_map.85 = (bf16[256,512]{1,0:T(8,128)(2,1)S(1)}, bf16[256,256]{1,0:T(8,128)(2,1)S(1)}, bf16[256,256]{1,0:T(8,128)(2,1)S(1)}, bf16[256,256]{1,0:T(8,128)(2,1)S(1)}, f32[256,512]{1,0:T(8,128)S(1)}) custom-call(bf16[256,512]{1,0:T(8,128)(2,1)} %feats_r.3, bf16[256,256]{1,0:T(8,128)(2,1)} %adj_r.3, bf16[256,256]{1,0:T(8,128)(2,1)} %couple_r.3, s32[1,256]{1,0:T(1,128)} %sr_r.1), custom_call_target="tpu_custom_call" | custom-call | tf_op jit(solution)/shard_map/pallas_call | solution.py:60
  42.8 1.9 %shard_map.87 = (bf16[2,256,512]{2,1,0:T(8,128)(2,1)S(1)}, bf16[256,512]{1,0:T(8,128)(2,1)S(1)}, f32[256,512]{1,0:T(8,128)S(1)}, bf16[256,512]{1,0:T(8,128)(2,1)...) custom-call(bf16[256,512]{1,0:T(8,128)(2,1)S(1)} %get-tuple-element., ...), custom_call_target="tpu_custom_call" | custom-call | tf_op jit(solution)/shard_map/pallas_call | solution.py:60
  44.7 1.5 %collective-permute-done.7.sr_r = s32[1,256]{1,0:T(1,128)S(1)} collective-permute-done((s32[1,256]{1,0:T(1,128)}, s32[1,256]{1,0:T(1,128)S(1)}, u32[]{:S(2)}, u32[]{:S(2)}) %collective-permute-start.7) | collective-permute-done | bytes 1056 | tf_op jit(solution)/shard_map/ppermute | solution.py:18
  46.2 1.4 %shard_map.88 = (f32[256,512]{1,0:T(8,128)S(1)}, bf16[3,256,512]{2,1,0:T(8,128)(2,1)S(1)}, f32[3,256,512]{2,1,0:T(8,128)S(1)}, bf16[3,256,512]{2,1,0:T(8,128)(2,...) custom-call(bf16[2,256,512]{2,1,0:T(8,128)(2,1)S(1)} %get-tuple-element.48., ...), custom_call_target="tpu_custom_call" | custom-call | tf_op jit(solution)/shard_map/pallas_call | solution.py:60
  47.6 0.0 copy-start
  47.6 2.3 %shard_map.89 = (bf16[256,512]{1,0:T(8,128)(2,1)}, bf16[1,4,256,512]{3,2,1,0:T(8,128)(2,1)S(1)}, f32[1,4,256,512]{3,2,1,0:T(8,128)S(1)}) custom-call(f32[3,256,512]{2,1,0:T(8,128)S(1)} %get-tuple-element.47.first_r, f32[256,512]{1,0:T(8,128)S(1)} %get-tuple-element.53.first3_r, bf16[256,512]{1,0:T(8,128)(2,1)S(1)} %get-tuple-element.54.x1_r, ...), custom_call_target="tpu_custom_call" | custom-call | tf_op jit(solution)/shard_map/pallas_call | solution.py:60
  49.9 1.4 %shard_map.90 = (bf16[768,512]{1,0:T(8,128)(2,1)S(1)}, f32[4,256,512]{2,1,0:T(8,128)S(1)}, f32[256,512]{1,0:T(8,128)S(1)}) custom-call(bf16[256,512]{1,0:T(8,128)(2,1)S(1)} %copy-done, bf16[2,512,512]{2,1,0:T(8,128)(2,1)S(1)} %get-tuple-element.64.w_r, f32[1,4,256,512]{3,2,1,0:T(8,128)S(1)} %get-tuple-element.65.slope_r.later_slope_r, ...), custom_call_target="tpu_custom_call" | custom-call | tf_op jit(solution)/shard_map/pallas_call | solution.py:60
  51.3 1.4 %shard_map.91 = (bf16[1024,512]{1,0:T(8,128)(2,1)S(1)}, f32[256,512]{1,0:T(8,128)S(1)}, f32[32,512]{1,0:T(8,128)S(1)}, bf16[32,512]{1,0:T(8,128)(2,1)S(1)}, bf16...) custom-call(bf16[768,512]{1,0:T(8,128)(2,1)S(1)} %get-tuple-element.67.dps_r, ...), custom_call_target="tpu_custom_call" | custom-call | tf_op jit(solution)/shard_map/pallas_call | solution.py:60
  52.7 1.6 %collective-permute-start.16 = (bf16[32,512]{1,0:T(8,128)(2,1)S(1)}, bf16[32,512]{1,0:T(8,128)(2,1)S(1)}, u32[]{:S(2)}, u32[]{:S(2)}) collective-permute-start(bf16[32,512]{1,0:T(8,128)(2,1)S(1)} %get-tuple-element.76), channel_id=1, source_target_pairs={{0,4},{2,6},{4,0},{6,2},{8,12},{10,14},{12,8},{14,10},{16,20},{18,... | collective-permute-start | bytes 98312 | tf_op jit(solution)/shard_map/ppermute | solution.py:18
  54.3 4.0 %collective-permute-start.17 = (bf16[32,512]{1,0:T(8,128)(2,1)S(1)}, bf16[32,512]{1,0:T(8,128)(2,1)S(1)}, u32[]{:S(2)}, u32[]{:S(2)}) collective-permute-start(bf16[32,512]{1,0:T(8,128)(2,1)S(1)} %get-tuple-element.77), channel_id=1, source_target_pairs={{0,8},{2,10},{4,12},{6,14},{8,0},{10,2},{12,4},{14,6},{16,24},{18,... | collective-permute-start | bytes 98312 | tf_op jit(solution)/shard_map/ppermute | solution.py:18
  58.3 1.4 %shard_map.92 = f32[256,256]{1,0:T(8,128)} custom-call(bf16[1024,512]{1,0:T(8,128)(2,1)S(1)} %get-tuple-element.79.dpre_r, f32[256,512]{1,0:T(8,128)S(1)} %get-tuple-element.80.carry_r, bf16[2,512,512]{2,1,0:T(8,128)(2,1)S(1)} %get-tuple-element.64.w_r, bf16[256,256]{1,0:T(8,128)(2,1)S(1)} %get-tuple-element.56.refs_0_, ...), custom_call_target="tpu_custom_call" | custom-call | tf_op jit(solution)/shard_map/pallas_call | solution.py:60
  59.7 0.5 collective-permute-done.17
  60.2 2.9 %collective-permute-done.18 = bf16[32,512]{1,0:T(8,128)(2,1)S(1)} collective-permute-done((bf16[32,512]{1,0:T(8,128)(2,1)S(1)}, bf16[32,512]{1,0:T(8,128)(2,1)S(1)}, u32[]{:S(2)}, u32[]{:S(2)}) %collective-permute-start.18) | collective-permute-done | bytes 32800 | tf_op jit(solution)/shard_map/ppermute | solution.py:18
  63.1 0.6 %add_bitcast_fusion = f32[1,32,512]{2,1,0:T(8,128)} fusion(bf16[32,512]{1,0:T(8,128)(2,1)S(1)} %collective-permute-done.18, bf16[32,512]{1,0:T(8,128)(2,1)S(1)} %collective-permute-done.17, f32[32,512]{1,0:T(8,128)S(1)} %get-tuple-element.75, bf16[32,512]{1,0:T(8,128)(2,1)S(1)} %collective-permute-done.16), kind=kLoop, calls=%fused_computation | loop fusion | flops 98304 | bytes 229376 | tf_op jit(solution)/shard_map/broadcast_in_dim | solution.py:556
  (17 shorter events, 0.0 us)
Async XLA Ops:
  1.7 16.1 %collective-permute-start.4 = (bf16[256,512]{1,0:T(8,128)(2,1)S(1)}, bf16[256,512]{1,0:T(8,128)(2,1)S(1)}, u32[]{:S(2)}, u32[]{:S(2)}) collective-permute-start(bf16[256,512]{1,0:T(8,128)(2,1)S(1)} %get-tuple-element.46), channel_id=1, source_target_pairs={{0,16},{2,18},{4,20},{6,22},{8,24},{10,26},{12,28},{14,30},{16,0},... | collective-permute-start | bytes 786440 | tf_op jit(solution)/shard_map/ppermute | solution.py:18
  5.9 25.4 %collective-permute-start.2 = (bf16[256,512]{1,0:T(8,128)(2,1)S(1)}, bf16[256,512]{1,0:T(8,128)(2,1)S(1)}, u32[]{:S(2)}, u32[]{:S(2)}) collective-permute-start(bf16[256,512]{1,0:T(8,128)(2,1)S(1)} %get-tuple-element.46), channel_id=1, source_target_pairs={{0,2},{2,0},{4,6},{6,4},{8,10},{10,8},{12,14},{14,12},{16,18},{18,... | collective-permute-start | bytes 786440 | tf_op jit(solution)/shard_map/ppermute | solution.py:18
  7.3 33.2 %collective-permute-start.6 = (bf16[512,512]{1,0:T(8,128)(2,1)}, bf16[512,512]{1,0:T(8,128)(2,1)S(1)}, u32[]{:S(2)}, u32[]{:S(2)}) collective-permute-start(bf16[512,512]{1,0:T(8,128)(2,1)} %refs_4_.1), channel_id=1, source_target_pairs={{0,1},{1,0},{2,3},{3,2},{4,5},{5,4},{6,7},{7,6},{8,9},{9,8},{10,11... | collective-permute-start | bytes 1572872 | tf_op jit(solution)/shard_map/ppermute | solution.py:23
  17.8 14.0 %collective-permute-start.8 = (bf16[256,512]{1,0:T(8,128)(2,1)S(1)}, bf16[256,512]{1,0:T(8,128)(2,1)S(1)}, u32[]{:S(2)}, u32[]{:S(2)}) collective-permute-start(bf16[256,512]{1,0:T(8,128)(2,1)S(1)} %collective-permute-done.4.refs_2_), channel_id=1, source_target_pairs={{0,2},{2,0},{4,6},{6,4},{8,10},{10,8},{12,14},{14,12},{16,18},{18,... | collective-permute-start | bytes 786440 | tf_op jit(solution)/shard_map/ppermute | solution.py:18
  19.3 12.0 %collective-permute-start.12 = (bf16[128,512]{1,0:T(8,128)(2,1)S(1)}, bf16[128,512]{1,0:T(8,128)(2,1)S(1)}, u32[]{:S(2)}, u32[]{:S(2)}) collective-permute-start(bf16[128,512]{1,0:T(8,128)(2,1)S(1)} %get-tuple-element.66), channel_id=1, source_target_pairs={{0,16},{2,18},{4,20},{6,22},{8,24},{10,26},{12,28},{14,30},{16,0},... | collective-permute-start | bytes 393224 | tf_op jit(solution)/shard_map/ppermute | solution.py:18
  19.3 6.0 %collective-permute-start = (s32[1,256]{1,0:T(1,128)}, s32[1,256]{1,0:T(1,128)S(1)}, u32[]{:S(2)}, u32[]{:S(2)}) collective-permute-start(s32[1,256]{1,0:T(1,128)} %sr_r.1), channel_id=1, source_target_pairs={{0,2},{2,0},{4,6},{6,4},{8,10},{10,8},{12,14},{14,12},{16,18},{18,... | collective-permute-start | bytes 3080 | tf_op jit(solution)/shard_map/ppermute | solution.py:18
  25.3 4.7 %collective-permute-start.1 = (s32[1,256]{1,0:T(1,128)}, s32[1,256]{1,0:T(1,128)S(1)}, u32[]{:S(2)}, u32[]{:S(2)}) collective-permute-start(s32[1,256]{1,0:T(1,128)} %sr_r.1), channel_id=1, source_target_pairs={{0,16},{2,18},{4,20},{6,22},{8,24},{10,26},{12,28},{14,30},{16,0},... | collective-permute-start | bytes 3080 | tf_op jit(solution)/shard_map/ppermute | solution.py:18
  30.0 5.0 %collective-permute-start.10 = (bf16[128,512]{1,0:T(8,128)(2,1)S(1)}, bf16[128,512]{1,0:T(8,128)(2,1)S(1)}, u32[]{:S(2)}, u32[]{:S(2)}) collective-permute-start(bf16[128,512]{1,0:T(8,128)(2,1)S(1)} %get-tuple-element.66), channel_id=1, source_target_pairs={{0,2},{2,0},{4,6},{6,4},{8,10},{10,8},{12,14},{14,12},{16,18},{18,... | collective-permute-start | bytes 393224 | tf_op jit(solution)/shard_map/ppermute | solution.py:18
  31.3 8.7 %collective-permute-start.5 = (bf16[256,512]{1,0:T(8,128)(2,1)S(1)}, bf16[256,512]{1,0:T(8,128)(2,1)S(1)}, u32[]{:S(2)}, u32[]{:S(2)}) collective-permute-start(bf16[256,512]{1,0:T(8,128)(2,1)S(1)} %collective-permute-done.4.refs_2_), channel_id=1, source_target_pairs={{0,1},{1,0},{2,3},{3,2},{4,5},{5,4},{6,7},{7,6},{8,9},{9,8},{10,11... | collective-permute-start | bytes 786440 | tf_op jit(solution)/shard_map/ppermute | solution.py:23
  31.3 9.2 %collective-permute-start.3 = (bf16[256,512]{1,0:T(8,128)(2,1)S(1)}, bf16[256,512]{1,0:T(8,128)(2,1)S(1)}, u32[]{:S(2)}, u32[]{:S(2)}) collective-permute-start(bf16[256,512]{1,0:T(8,128)(2,1)S(1)} %collective-permute-done.2.refs_0_), channel_id=1, source_target_pairs={{0,1},{1,0},{2,3},{3,2},{4,5},{5,4},{6,7},{7,6},{8,9},{9,8},{10,11... | collective-permute-start | bytes 786440 | tf_op jit(solution)/shard_map/ppermute | solution.py:23
  31.8 14.4 %collective-permute-start.9 = (bf16[256,512]{1,0:T(8,128)(2,1)S(1)}, bf16[256,512]{1,0:T(8,128)(2,1)S(1)}, u32[]{:S(2)}, u32[]{:S(2)}) collective-permute-start(bf16[256,512]{1,0:T(8,128)(2,1)S(1)} %collective-permute-done.8.refs_0_), channel_id=1, source_target_pairs={{0,1},{1,0},{2,3},{3,2},{4,5},{5,4},{6,7},{7,6},{8,9},{9,8},{10,11... | collective-permute-start | bytes 786440 | tf_op jit(solution)/shard_map/ppermute | solution.py:23
  35.0 5.0 %collective-permute-start.14 = (bf16[128,512]{1,0:T(8,128)(2,1)S(1)}, bf16[128,512]{1,0:T(8,128)(2,1)S(1)}, u32[]{:S(2)}, u32[]{:S(2)}) collective-permute-start(bf16[128,512]{1,0:T(8,128)(2,1)S(1)} %collective-permute-done.12.refs_9_), channel_id=1, source_target_pairs={{0,2},{2,0},{4,6},{6,4},{8,10},{10,8},{12,14},{14,12},{16,18},{18,... | collective-permute-start | bytes 393224 | tf_op jit(solution)/shard_map/ppermute | solution.py:18
  40.0 9.9 %collective-permute-start.13 = (bf16[128,512]{1,0:T(8,128)(2,1)S(1)}, bf16[128,512]{1,0:T(8,128)(2,1)S(1)}, u32[]{:S(2)}, u32[]{:S(2)}) collective-permute-start(bf16[128,512]{1,0:T(8,128)(2,1)S(1)} %collective-permute-done.12.refs_9_), channel_id=1, source_target_pairs={{0,1},{1,0},{2,3},{3,2},{4,5},{5,4},{6,7},{7,6},{8,9},{9,8},{10,11... | collective-permute-start | bytes 393224 | tf_op jit(solution)/shard_map/ppermute | solution.py:23
  40.0 9.9 %collective-permute-start.11 = (bf16[128,512]{1,0:T(8,128)(2,1)S(1)}, bf16[128,512]{1,0:T(8,128)(2,1)S(1)}, u32[]{:S(2)}, u32[]{:S(2)}) collective-permute-start(bf16[128,512]{1,0:T(8,128)(2,1)S(1)} %collective-permute-done.10.refs_7_), channel_id=1, source_target_pairs={{0,1},{1,0},{2,3},{3,2},{4,5},{5,4},{6,7},{7,6},{8,9},{9,8},{10,11... | collective-permute-start | bytes 393224 | tf_op jit(solution)/shard_map/ppermute | solution.py:23
  40.5 10.8 %collective-permute-start.15 = (bf16[128,512]{1,0:T(8,128)(2,1)S(1)}, bf16[128,512]{1,0:T(8,128)(2,1)S(1)}, u32[]{:S(2)}, u32[]{:S(2)}) collective-permute-start(bf16[128,512]{1,0:T(8,128)(2,1)S(1)} %collective-permute-done.14.refs_7_), channel_id=1, source_target_pairs={{0,1},{1,0},{2,3},{3,2},{4,5},{5,4},{6,7},{7,6},{8,9},{9,8},{10,11... | collective-permute-start | bytes 393224 | tf_op jit(solution)/shard_map/ppermute | solution.py:23
  40.6 5.6 %collective-permute-start.7 = (s32[1,256]{1,0:T(1,128)}, s32[1,256]{1,0:T(1,128)S(1)}, u32[]{:S(2)}, u32[]{:S(2)}) collective-permute-start(s32[1,256]{1,0:T(1,128)} %sr_r.1), channel_id=1, source_target_pairs={{0,18},{2,16},{4,22},{6,20},{8,26},{10,24},{12,30},{14,28},{16,2},... | collective-permute-start | bytes 3080 | tf_op jit(solution)/shard_map/ppermute | solution.py:18
  47.6 2.3 %copy-start = (bf16[256,512]{1,0:T(8,128)(2,1)S(1)}, bf16[256,512]{1,0:T(8,128)(2,1)}, u32[]{:S(2)}) copy-start(bf16[256,512]{1,0:T(8,128)(2,1)} %cot_r.3) | copy-start | bytes 786436
  52.7 7.0 %collective-permute-start.16 = (bf16[32,512]{1,0:T(8,128)(2,1)S(1)}, bf16[32,512]{1,0:T(8,128)(2,1)S(1)}, u32[]{:S(2)}, u32[]{:S(2)}) collective-permute-start(bf16[32,512]{1,0:T(8,128)(2,1)S(1)} %get-tuple-element.76), channel_id=1, source_target_pairs={{0,4},{2,6},{4,0},{6,2},{8,12},{10,14},{12,8},{14,10},{16,20},{18,... | collective-permute-start | bytes 98312 | tf_op jit(solution)/shard_map/ppermute | solution.py:18
  54.3 5.9 %collective-permute-start.17 = (bf16[32,512]{1,0:T(8,128)(2,1)S(1)}, bf16[32,512]{1,0:T(8,128)(2,1)S(1)}, u32[]{:S(2)}, u32[]{:S(2)}) collective-permute-start(bf16[32,512]{1,0:T(8,128)(2,1)S(1)} %get-tuple-element.77), channel_id=1, source_target_pairs={{0,8},{2,10},{4,12},{6,14},{8,0},{10,2},{12,4},{14,6},{16,24},{18,... | collective-permute-start | bytes 98312 | tf_op jit(solution)/shard_map/ppermute | solution.py:18
  58.3 4.8 %collective-permute-start.18 = (bf16[32,512]{1,0:T(8,128)(2,1)S(1)}, bf16[32,512]{1,0:T(8,128)(2,1)S(1)}, u32[]{:S(2)}, u32[]{:S(2)}) collective-permute-start(bf16[32,512]{1,0:T(8,128)(2,1)S(1)} %get-tuple-element.78), channel_id=1, source_target_pairs={{0,12},{2,14},{4,8},{6,10},{8,4},{10,6},{12,0},{14,2},{16,28},{18,... | collective-permute-start | bytes 98312 | tf_op jit(solution)/shard_map/ppermute | solution.py:18

commit v2 on v1

--- a/solution.py
+++ b/solution.py
@@ -238,7 +238,7 @@
 
     def body(x12_r, sums_r, cp_r, pick_r, w_r, first_r, sr_r, *refs):
         got_r = refs[:layers]
-        first3_o, x3_s, mix_o, slope_o, x1_o, own3_o, near23_o, far13_o, ac_s = (refs[layers], refs[-1], *refs[layers + 1 : -1])
+        first3_o, x3_s, mix_o, slope_o, x1_o, own3_o, near23_o, far13_o, back3_o, ac_s = (refs[layers], refs[-1], *refs[layers + 1 : -1])
         seg = lax.axis_index("segment")
         for k in range(layers):
             at = piece_slice(seg, k, layers, piece)
@@ -251,6 +251,9 @@
         near23_o[0] = mm_nt(cp_r[1], picks[:, :bound]).astype(BF16)
         near23_o[1] = mm_nt(ac_s[:, :bound], pick_r[1]).astype(BF16)
         far13_o[1] = mm_nt(ac_s[:, bound:], pick_r[0]).astype(BF16)
+        back3_o[0] = mm_nt(pick_r[0], ac_s[:, bound:]).astype(BF16)
+        back3_o[1] = mm_nt(pick_r[1], ac_s[:, :bound]).astype(BF16)
+        back3_o[2] = own3_o[...].T
         for g in range(3):
             if g < 2:
                 agg = sums_r[g] + mm((far13_o, near23_o)[g][0], x3_s[...])
@@ -272,6 +275,7 @@
             sds((rows, rows), BF16),
             sds((2, rows, rows), BF16),
             sds((2, rows, rows), BF16),
+            sds((3, rows, rows), BF16),
         ),
         [(a, "v") for a in (x12, sums, cp, pick, w, first, diag_sr, *diag)],
         [pltpu.VMEM((rows, 2 * bound), BF16), pltpu.VMEM((rows, width), BF16)],
@@ -313,20 +317,26 @@
 
         for k in range(1, layers):
             dst = (xa_s, xb_s)[k % 2]
-            for g in range(4):
-                agg = mm(along(1, own_at(g), near_at(g), far_at(g)), along(0, src(g), src(g ^ 1), src(g ^ 2)))
-                mixed = mixed_of(agg, first_r[g] if g < 3 else first3_r[...])
-                mix_o[k - 1, g] = mixed
-            through = mm(along(0, *[mix_o[k - 1, g] for g in range(4)]), w_r[k])
-            for g in range(4):
-                slope_o[k - 1, g], out = activate(mix_o[k - 1, g], through[g * rows : (g + 1) * rows], k)
-                if k + 1 < layers:
-                    dst[g] = out
-                if g == 0:
-
-                    @pl.when(seg == k)
-                    def _():
-                        acts_o[...] = out
+            own_out = {}
+            for some in ((0, 1, 2, 3),):
+                for g in some:
+                    agg = mm(along(1, own_at(g), near_at(g), far_at(g)), along(0, src(g), src(g ^ 1), src(g ^ 2)))
+                    mix_o[k - 1, g] = mixed_of(agg, first_r[g] if g < 3 else first3_r[...])
+                for c in range(2):
+                    at = slice(c * width // 2, (c + 1) * width // 2)
+                    through = mm(along(0, *[mix_o[k - 1, g] for g in some]), w_r[k, :, at])
+                    for i, g in enumerate(some):
+                        out = activate(mix_o[k - 1, g, :, at], through[i * rows : (i + 1) * rows], k)
+                        slope_o[k - 1, g, :, at] = out[0]
+                        if k + 1 < layers:
+                            dst[g, :, at] = out[1]
+                        if g == 0:
+                            own_out[c] = out[1]
+            for c in range(2):
+
+                @pl.when(seg == k)
+                def _():
+                    acts_o[:, c * width // 2 : (c + 1) * width // 2] = own_out[c]
 
             def src(g, dst=dst):
                 return dst[g]
@@ -401,7 +411,7 @@
     m = len(arrays)
     last = layers - 1
 
-    def body(dps_r, sums_r, carry_r, mix_r, slope_r, mixn_r, slopen_r, later_mix_r, later_slope_r, w_r, *refs):
+    def body(dps_r, sums_r, carry_r, mix_r, slope_r, mixn_r, slopen_r, later_mix_r, later_slope_r, w_r, back3_r, *refs):
         own_at, near_at, far_at = readers(refs[:m])
         got_r = refs[m : m + layers]
         outs = refs[m + layers :]
@@ -420,7 +430,7 @@
         dpre = ((0.5 * up_s[3]).astype(F32) * later_slope_r[last - 1, 3]).astype(BF16)
         dpre_o[pl.ds(3 * rows, rows), :] = dpre
         dmix = dmix_of(dpre, w_r[last], last)
-        extra = (None, mm_tn(far_at(3), dmix), mm_tn(near_at(3), dmix), mm_tn(own_at(3), dmix))
+        extra = (None, *[mm(back3_r[n], dmix) for n in range(3)])
         for g in range(4):
             total = sums_r[g] if g == 0 else sums_r[g] + extra[g]
             up_s[g] = ((0.5 - 0.5 * SHARE) * total).astype(BF16)
@@ -477,6 +487,7 @@
                 later_mix,
                 later_slope,
                 w,
+                rest[7],
                 *arrays,
                 *diag,
             )
@@ -491,7 +502,7 @@
     return got[0], got[1], got[2], got[3:]
 
 
-def feat_call(dpre, carry, w, matrix):
+def feat_call(dpre, carry, w, acts, matrix):
     arrays, readers = matrix
     layers = w.shape[0]
     rows, width = carry.shape
@@ -501,9 +512,10 @@
     m = len(arrays)
     beta = beta_of(0)
 
-    def body(dpre_r, carry_r, w_r, *refs):
+    def body(dpre_r, carry_r, w_r, acts_r, *refs):
         own_at, near_at, far_at = readers(refs[:m])
-        feat_o = refs[m]
+        feat_o, acts_o = refs[m:]
+        acts_o[...] = acts_r[...]
         at = pl.ds(pl.multiple_of(lax.axis_index("segment") * cols, cols), cols) if sliced else slice(None)
         w_cols = w_r[0, :, at]
         dmix = []
@@ -514,8 +526,14 @@
         sums = mm_tn(along(0, own_at(0), near_at(1), far_at(2)), along(0, *dmix))
         feat_o[...] = (1.0 - SHARE) * sums + (carry_r[:, at] + SHARE * dmix[0].astype(F32))
 
-    (feat,) = call(body, (sds((rows, kept), F32),), [(a, "v") for a in (dpre, carry, w, *arrays)], vmem=12)
-    return feat if sliced else lax.dynamic_slice_in_dim(feat, lax.axis_index("segment") * cols, cols, 1)
+    feat, acts = call(
+        body,
+        (sds((rows, kept), F32), sds(acts.shape, acts.dtype)),
+        [(a, "v") for a in (dpre, carry, w, acts, *arrays)],
+        vmem=12,
+    )
+    feat = feat if sliced else lax.dynamic_slice_in_dim(feat, lax.axis_index("segment") * cols, cols, 1)
+    return feat, acts
 
 
 def step(feats, adj, couple, send_rows, weights, cot):
@@ -552,7 +570,7 @@
     )
     for m in range(1, others):
         wgrad = wgrad + swapped(sends[m - 1], 2 * m).astype(F32)
-    feat = feat_call(dpre, carry, w_t, matrix)
+    feat, acts = feat_call(dpre, carry, w_t, acts, matrix)
     return (acts[None], wgrad[None], feat)
 
 

time: 64 us -> 63.7 us (level)
  no operation moved by 1% of the time
where the time goes in v2:
time: 63.7 us; the launch traced here: 63.5 us
  waiting for transfers between devices  31.1 us (49%)
  starting transfers between devices  19.1 us (30%)
  Pallas kernels  11.9 us (19%)
  between operations  0.74 us (1%)
  other arithmetic  0.65 us (1%)
    ppermute x12, waiting for transfers between devices, swapped(): lax.ppermute(x, 'dom', [(i, i ^ mask) for i in range(lax.axis_size('dom'))])  31 us
    ppermute x12, starting transfers between devices, swapped(): lax.ppermute(x, 'dom', [(i, i ^ mask) for i in range(lax.axis_size('dom'))])  18 us
    pallas_call x8, Pallas kernels, call(): pl.pallas_call(body, out_shape=tuple(out_shape), in_specs=specs, out_spec...  11.9 us
  transfers between devices with their start and end apart: 19, of which 8 were waited for; matrix products, arithmetic and copies ran while one was open for 0% of the time, Pallas kernels for 15%

profile of v2, /device:TPU:0, one launch (start us, length us, event | category | flops | bytes accessed | tf_op | source)
XLA Modules:
  0.0 63.5 jit_solution(2170449316544541096)
XLA Ops:
  0.6 1.1 %shard_map.86 = (bf16[256,512]{1,0:T(8,128)(2,1)S(1)}, bf16[128,512]{1,0:T(8,128)(2,1)S(1)}) custom-call(bf16[256,512]{1,0:T(8,128)(2,1)} %feats_r.3, bf16[256,256]{1,0:T(8,128)(2,1)} %adj_r.3, bf16[256,256]{1,0:T(8,128)(2,1)} %couple_r.3, bf16[256,512]{1,0:T(8,128)(2,1)} %cot_r.3), custom_call_target="tpu_custom_call" | custom-call | tf_op jit(solution)/shard_map/pallas_call | solution.py:60
  1.7 4.1 %collective-permute-start.4 = (bf16[256,512]{1,0:T(8,128)(2,1)S(1)}, bf16[256,512]{1,0:T(8,128)(2,1)S(1)}, u32[]{:S(2)}, u32[]{:S(2)}) collective-permute-start(bf16[256,512]{1,0:T(8,128)(2,1)S(1)} %get-tuple-element.49), channel_id=1, source_target_pairs={{0,16},{2,18},{4,20},{6,22},{8,24},{10,26},{12,28},{14,30},{16,0},... | collective-permute-start | bytes 786440 | tf_op jit(solution)/shard_map/ppermute | solution.py:18
  5.9 1.5 %collective-permute-start.2 = (bf16[256,512]{1,0:T(8,128)(2,1)S(1)}, bf16[256,512]{1,0:T(8,128)(2,1)S(1)}, u32[]{:S(2)}, u32[]{:S(2)}) collective-permute-start(bf16[256,512]{1,0:T(8,128)(2,1)S(1)} %get-tuple-element.49), channel_id=1, source_target_pairs={{0,2},{2,0},{4,6},{6,4},{8,10},{10,8},{12,14},{14,12},{16,18},{18,... | collective-permute-start | bytes 786440 | tf_op jit(solution)/shard_map/ppermute | solution.py:18
  7.3 10.4 %collective-permute-done.4.refs_2_ = bf16[256,512]{1,0:T(8,128)(2,1)S(1)} collective-permute-done((bf16[256,512]{1,0:T(8,128)(2,1)S(1)}, bf16[256,512]{1,0:T(8,128)(2,1)S(1)}, u32[]{:S(2)}, u32[]{:S(2)}) %collective-permute-start.4) | collective-permute-done | bytes 262176 | tf_op jit(solution)/shard_map/ppermute | solution.py:18
  17.8 1.5 %collective-permute-start.8 = (bf16[256,512]{1,0:T(8,128)(2,1)S(1)}, bf16[256,512]{1,0:T(8,128)(2,1)S(1)}, u32[]{:S(2)}, u32[]{:S(2)}) collective-permute-start(bf16[256,512]{1,0:T(8,128)(2,1)S(1)} %collective-permute-done.4.refs_2_), channel_id=1, source_target_pairs={{0,2},{2,0},{4,6},{6,4},{8,10},{10,8},{12,14},{14,12},{16,18},{18,... | collective-permute-start | bytes 786440 | tf_op jit(solution)/shard_map/ppermute | solution.py:18
  19.3 0.5 collective-permute-start
  19.8 5.5 %collective-permute-done.near_sr_r = s32[1,256]{1,0:T(1,128)S(1)} collective-permute-done((s32[1,256]{1,0:T(1,128)}, s32[1,256]{1,0:T(1,128)S(1)}, u32[]{:S(2)}, u32[]{:S(2)}) %collective-permute-start) | collective-permute-done | bytes 1056 | tf_op jit(solution)/shard_map/ppermute | solution.py:18
  25.3 0.7 %collective-permute-start.1 = (s32[1,256]{1,0:T(1,128)}, s32[1,256]{1,0:T(1,128)S(1)}, u32[]{:S(2)}, u32[]{:S(2)}) collective-permute-start(s32[1,256]{1,0:T(1,128)} %sr_r.1), channel_id=1, source_target_pairs={{0,16},{2,18},{4,20},{6,22},{8,24},{10,26},{12,28},{14,30},{16,0},... | collective-permute-start | bytes 3080 | tf_op jit(solution)/shard_map/ppermute | solution.py:18
  26.0 4.0 %collective-permute-done.1.far_sr_r = s32[1,256]{1,0:T(1,128)S(1)} collective-permute-done((s32[1,256]{1,0:T(1,128)}, s32[1,256]{1,0:T(1,128)S(1)}, u32[]{:S(2)}, u32[]{:S(2)}) %collective-permute-start.1) | collective-permute-done | bytes 1056 | tf_op jit(solution)/shard_map/ppermute | solution.py:18
  30.0 1.3 %collective-permute-start.10 = (bf16[128,512]{1,0:T(8,128)(2,1)S(1)}, bf16[128,512]{1,0:T(8,128)(2,1)S(1)}, u32[]{:S(2)}, u32[]{:S(2)}) collective-permute-start(bf16[128,512]{1,0:T(8,128)(2,1)S(1)} %get-tuple-element.68), channel_id=1, source_target_pairs={{0,2},{2,0},{4,6},{6,4},{8,10},{10,8},{12,14},{14,12},{16,18},{18,... | collective-permute-start | bytes 393224 | tf_op jit(solution)/shard_map/ppermute | solution.py:18
  31.3 0.5 collective-permute-start.3
  31.8 0.1 collective-permute-start.9
  31.9 3.1 %collective-permute-done.10.refs_7_ = bf16[128,512]{1,0:T(8,128)(2,1)S(1)} collective-permute-done((bf16[128,512]{1,0:T(8,128)(2,1)S(1)}, bf16[128,512]{1,0:T(8,128)(2,1)S(1)}, u32[]{:S(2)}, u32[]{:S(2)}) %collective-permute-start.10) | collective-permute-done | bytes 131104 | tf_op jit(solution)/shard_map/ppermute | solution.py:18
  35.0 1.8 %collective-permute-start.14 = (bf16[128,512]{1,0:T(8,128)(2,1)S(1)}, bf16[128,512]{1,0:T(8,128)(2,1)S(1)}, u32[]{:S(2)}, u32[]{:S(2)}) collective-permute-start(bf16[128,512]{1,0:T(8,128)(2,1)S(1)} %collective-permute-done.12.refs_9_), channel_id=1, source_target_pairs={{0,2},{2,0},{4,6},{6,4},{8,10},{10,8},{12,14},{14,12},{16,18},{18,... | collective-permute-start | bytes 393224 | tf_op jit(solution)/shard_map/ppermute | solution.py:18
  36.8 3.1 %collective-permute-done.14.refs_7_ = bf16[128,512]{1,0:T(8,128)(2,1)S(1)} collective-permute-done((bf16[128,512]{1,0:T(8,128)(2,1)S(1)}, bf16[128,512]{1,0:T(8,128)(2,1)S(1)}, u32[]{:S(2)}, u32[]{:S(2)}) %collective-permute-start.14) | collective-permute-done | bytes 131104 | tf_op jit(solution)/shard_map/ppermute | solution.py:18
  40.0 0.5 collective-permute-start.11
  40.5 0.1 collective-permute-start.15
  40.6 0.9 %collective-permute-start.7 = (s32[1,256]{1,0:T(1,128)}, s32[1,256]{1,0:T(1,128)S(1)}, u32[]{:S(2)}, u32[]{:S(2)}) collective-permute-start(s32[1,256]{1,0:T(1,128)} %sr_r.1), channel_id=1, source_target_pairs={{0,18},{2,16},{4,22},{6,20},{8,26},{10,24},{12,30},{14,28},{16,2},... | collective-permute-start | bytes 3080 | tf_op jit(solution)/shard_map/ppermute | solution.py:18
  41.4 1.3 %shard_map.85 = (bf16[256,512]{1,0:T(8,128)(2,1)S(1)}, bf16[256,256]{1,0:T(8,128)(2,1)S(1)}, bf16[256,256]{1,0:T(8,128)(2,1)S(1)}, bf16[256,256]{1,0:T(8,128)(2,1)S(1)}, f32[256,512]{1,0:T(8,128)S(1)}) custom-call(bf16[256,512]{1,0:T(8,128)(2,1)} %feats_r.3, bf16[256,256]{1,0:T(8,128)(2,1)} %adj_r.3, bf16[256,256]{1,0:T(8,128)(2,1)} %couple_r.3, s32[1,256]{1,0:T(1,128)} %sr_r.1), custom_call_target="tpu_custom_call" | custom-call | tf_op jit(solution)/shard_map/pallas_call | solution.py:60
  42.8 1.9 %shard_map.87 = (bf16[2,256,512]{2,1,0:T(8,128)(2,1)S(1)}, bf16[256,512]{1,0:T(8,128)(2,1)S(1)}, f32[256,512]{1,0:T(8,128)S(1)}, bf16[256,512]{1,0:T(8,128)(2,1)...) custom-call(bf16[256,512]{1,0:T(8,128)(2,1)S(1)} %get-tuple-element., ...), custom_call_target="tpu_custom_call" | custom-call | tf_op jit(solution)/shard_map/pallas_call | solution.py:60
  44.7 1.4 %collective-permute-done.7.sr_r = s32[1,256]{1,0:T(1,128)S(1)} collective-permute-done((s32[1,256]{1,0:T(1,128)}, s32[1,256]{1,0:T(1,128)S(1)}, u32[]{:S(2)}, u32[]{:S(2)}) %collective-permute-start.7) | collective-permute-done | bytes 1056 | tf_op jit(solution)/shard_map/ppermute | solution.py:18
  46.2 1.5 %shard_map.88 = (f32[256,512]{1,0:T(8,128)S(1)}, bf16[3,256,512]{2,1,0:T(8,128)(2,1)S(1)}, f32[3,256,512]{2,1,0:T(8,128)S(1)}, bf16[3,256,512]{2,1,0:T(8,128)(2,...) custom-call(bf16[2,256,512]{2,1,0:T(8,128)(2,1)S(1)} %get-tuple-elem, ...), custom_call_target="tpu_custom_call" | custom-call | tf_op jit(solution)/shard_map/pallas_call | solution.py:60
  47.7 0.0 copy-start
  47.7 1.9 %shard_map.89 = (bf16[256,512]{1,0:T(8,128)(2,1)S(1)}, bf16[1,4,256,512]{3,2,1,0:T(8,128)(2,1)S(1)}, f32[1,4,256,512]{3,2,1,0:T(8,128)S(1)}) custom-call(f32[3,256,512]{2,1,0:T(8,128)S(1)} %get-tuple-element.51.first_r, f32[256,512]{1,0:T(8,128)S(1)} %get-tuple-element.57.first3_r, bf16[256,512]{1,0:T(8,128)(2,1)S(1)} %get-tuple-element.58.x1_r, ...), custom_call_target="tpu_custom_call" | custom-call | tf_op jit(solution)/shard_map/pallas_call | solution.py:60
  49.6 1.4 %shard_map.90 = (bf16[768,512]{1,0:T(8,128)(2,1)S(1)}, f32[4,256,512]{2,1,0:T(8,128)S(1)}, f32[256,512]{1,0:T(8,128)S(1)}) custom-call(bf16[256,512]{1,0:T(8,128)(2,1)S(1)} %copy-done, bf16[2,512,512]{2,1,0:T(8,128)(2,1)S(1)} %get-tuple-element.50.w_r, f32[1,4,256,512]{3,2,1,0:T(8,128)S(1)} %get-tuple-element.67.slope_r.later_slope_r, ...), custom_call_target="tpu_custom_call" | custom-call | tf_op jit(solution)/shard_map/pallas_call | solution.py:60
  51.0 1.4 %shard_map.91 = (bf16[1024,512]{1,0:T(8,128)(2,1)S(1)}, f32[256,512]{1,0:T(8,128)S(1)}, f32[32,512]{1,0:T(8,128)S(1)}, bf16[32,512]{1,0:T(8,128)(2,1)S(1)}, bf16...) custom-call(bf16[768,512]{1,0:T(8,128)(2,1)S(1)} %get-tuple-element.69.dps_r, ...), custom_call_target="tpu_custom_call" | custom-call | tf_op jit(solution)/shard_map/pallas_call | solution.py:60
  52.4 1.6 %collective-permute-start.16 = (bf16[32,512]{1,0:T(8,128)(2,1)S(1)}, bf16[32,512]{1,0:T(8,128)(2,1)S(1)}, u32[]{:S(2)}, u32[]{:S(2)}) collective-permute-start(bf16[32,512]{1,0:T(8,128)(2,1)S(1)} %get-tuple-element.83), channel_id=1, source_target_pairs={{0,4},{2,6},{4,0},{6,2},{8,12},{10,14},{12,8},{14,10},{16,20},{18,... | collective-permute-start | bytes 98312 | tf_op jit(solution)/shard_map/ppermute | solution.py:18
  54.0 4.0 %collective-permute-start.17 = (bf16[32,512]{1,0:T(8,128)(2,1)S(1)}, bf16[32,512]{1,0:T(8,128)(2,1)S(1)}, u32[]{:S(2)}, u32[]{:S(2)}) collective-permute-start(bf16[32,512]{1,0:T(8,128)(2,1)S(1)} %get-tuple-element.84), channel_id=1, source_target_pairs={{0,8},{2,10},{4,12},{6,14},{8,0},{10,2},{12,4},{14,6},{16,24},{18,... | collective-permute-start | bytes 98312 | tf_op jit(solution)/shard_map/ppermute | solution.py:18
  58.0 1.4 %shard_map.92 = (f32[256,256]{1,0:T(8,128)}, bf16[256,512]{1,0:T(8,128)(2,1)}) custom-call(bf16[1024,512]{1,0:T(8,128)(2,1)S(1)} %get-tuple-element.78.dpre_r, f32[256,512]{1,0:T(8,128)S(1)} %get-tuple-element.79.carry_r, bf16[2,512,512]{2,1,0:T(8,128)(2,1)S(1)} %get-tuple-element.50.w_r, bf16[256,512]{1,0:T(8,128)(2,1)S(1)} %get-tuple-element.80.acts_r, ...), custom_call_target="tpu_custom_call" | custom-call | tf_op jit(solution)/shard_map/pallas_call | solution.py:60
  59.4 0.5 collective-permute-done.17
  59.9 2.9 %collective-permute-done.18 = bf16[32,512]{1,0:T(8,128)(2,1)S(1)} collective-permute-done((bf16[32,512]{1,0:T(8,128)(2,1)S(1)}, bf16[32,512]{1,0:T(8,128)(2,1)S(1)}, u32[]{:S(2)}, u32[]{:S(2)}) %collective-permute-start.18) | collective-permute-done | bytes 32800 | tf_op jit(solution)/shard_map/ppermute | solution.py:18
  62.8 0.6 %add_bitcast_fusion = f32[1,32,512]{2,1,0:T(8,128)} fusion(bf16[32,512]{1,0:T(8,128)(2,1)S(1)} %collective-permute-done.18, bf16[32,512]{1,0:T(8,128)(2,1)S(1)} %collective-permute-done.17, f32[32,512]{1,0:T(8,128)S(1)} %get-tuple-element.82, bf16[32,512]{1,0:T(8,128)(2,1)S(1)} %collective-permute-done.16), kind=kLoop, calls=%fused_computation | loop fusion | flops 98304 | bytes 229376 | tf_op jit(solution)/shard_map/broadcast_in_dim | solution.py:574
  (17 shorter events, 0.0 us)
Async XLA Ops:
  1.7 16.1 %collective-permute-start.4 = (bf16[256,512]{1,0:T(8,128)(2,1)S(1)}, bf16[256,512]{1,0:T(8,128)(2,1)S(1)}, u32[]{:S(2)}, u32[]{:S(2)}) collective-permute-start(bf16[256,512]{1,0:T(8,128)(2,1)S(1)} %get-tuple-element.49), channel_id=1, source_target_pairs={{0,16},{2,18},{4,20},{6,22},{8,24},{10,26},{12,28},{14,30},{16,0},... | collective-permute-start | bytes 786440 | tf_op jit(solution)/shard_map/ppermute | solution.py:18
  5.9 25.4 %collective-permute-start.2 = (bf16[256,512]{1,0:T(8,128)(2,1)S(1)}, bf16[256,512]{1,0:T(8,128)(2,1)S(1)}, u32[]{:S(2)}, u32[]{:S(2)}) collective-permute-start(bf16[256,512]{1,0:T(8,128)(2,1)S(1)} %get-tuple-element.49), channel_id=1, source_target_pairs={{0,2},{2,0},{4,6},{6,4},{8,10},{10,8},{12,14},{14,12},{16,18},{18,... | collective-permute-start | bytes 786440 | tf_op jit(solution)/shard_map/ppermute | solution.py:18
  7.3 33.2 %collective-permute-start.6 = (bf16[512,512]{1,0:T(8,128)(2,1)}, bf16[512,512]{1,0:T(8,128)(2,1)S(1)}, u32[]{:S(2)}, u32[]{:S(2)}) collective-permute-start(bf16[512,512]{1,0:T(8,128)(2,1)} %refs_4_.1), channel_id=1, source_target_pairs={{0,1},{1,0},{2,3},{3,2},{4,5},{5,4},{6,7},{7,6},{8,9},{9,8},{10,11... | collective-permute-start | bytes 1572872 | tf_op jit(solution)/shard_map/ppermute | solution.py:23
  17.8 14.0 %collective-permute-start.8 = (bf16[256,512]{1,0:T(8,128)(2,1)S(1)}, bf16[256,512]{1,0:T(8,128)(2,1)S(1)}, u32[]{:S(2)}, u32[]{:S(2)}) collective-permute-start(bf16[256,512]{1,0:T(8,128)(2,1)S(1)} %collective-permute-done.4.refs_2_), channel_id=1, source_target_pairs={{0,2},{2,0},{4,6},{6,4},{8,10},{10,8},{12,14},{14,12},{16,18},{18,... | collective-permute-start | bytes 786440 | tf_op jit(solution)/shard_map/ppermute | solution.py:18
  19.3 12.0 %collective-permute-start.12 = (bf16[128,512]{1,0:T(8,128)(2,1)S(1)}, bf16[128,512]{1,0:T(8,128)(2,1)S(1)}, u32[]{:S(2)}, u32[]{:S(2)}) collective-permute-start(bf16[128,512]{1,0:T(8,128)(2,1)S(1)} %get-tuple-element.68), channel_id=1, source_target_pairs={{0,16},{2,18},{4,20},{6,22},{8,24},{10,26},{12,28},{14,30},{16,0},... | collective-permute-start | bytes 393224 | tf_op jit(solution)/shard_map/ppermute | solution.py:18
  19.3 6.0 %collective-permute-start = (s32[1,256]{1,0:T(1,128)}, s32[1,256]{1,0:T(1,128)S(1)}, u32[]{:S(2)}, u32[]{:S(2)}) collective-permute-start(s32[1,256]{1,0:T(1,128)} %sr_r.1), channel_id=1, source_target_pairs={{0,2},{2,0},{4,6},{6,4},{8,10},{10,8},{12,14},{14,12},{16,18},{18,... | collective-permute-start | bytes 3080 | tf_op jit(solution)/shard_map/ppermute | solution.py:18
  25.3 4.7 %collective-permute-start.1 = (s32[1,256]{1,0:T(1,128)}, s32[1,256]{1,0:T(1,128)S(1)}, u32[]{:S(2)}, u32[]{:S(2)}) collective-permute-start(s32[1,256]{1,0:T(1,128)} %sr_r.1), channel_id=1, source_target_pairs={{0,16},{2,18},{4,20},{6,22},{8,24},{10,26},{12,28},{14,30},{16,0},... | collective-permute-start | bytes 3080 | tf_op jit(solution)/shard_map/ppermute | solution.py:18
  30.0 5.0 %collective-permute-start.10 = (bf16[128,512]{1,0:T(8,128)(2,1)S(1)}, bf16[128,512]{1,0:T(8,128)(2,1)S(1)}, u32[]{:S(2)}, u32[]{:S(2)}) collective-permute-start(bf16[128,512]{1,0:T(8,128)(2,1)S(1)} %get-tuple-element.68), channel_id=1, source_target_pairs={{0,2},{2,0},{4,6},{6,4},{8,10},{10,8},{12,14},{14,12},{16,18},{18,... | collective-permute-start | bytes 393224 | tf_op jit(solution)/shard_map/ppermute | solution.py:18
  31.3 8.7 %collective-permute-start.5 = (bf16[256,512]{1,0:T(8,128)(2,1)S(1)}, bf16[256,512]{1,0:T(8,128)(2,1)S(1)}, u32[]{:S(2)}, u32[]{:S(2)}) collective-permute-start(bf16[256,512]{1,0:T(8,128)(2,1)S(1)} %collective-permute-done.4.refs_2_), channel_id=1, source_target_pairs={{0,1},{1,0},{2,3},{3,2},{4,5},{5,4},{6,7},{7,6},{8,9},{9,8},{10,11... | collective-permute-start | bytes 786440 | tf_op jit(solution)/shard_map/ppermute | solution.py:23
  31.3 9.2 %collective-permute-start.3 = (bf16[256,512]{1,0:T(8,128)(2,1)S(1)}, bf16[256,512]{1,0:T(8,128)(2,1)S(1)}, u32[]{:S(2)}, u32[]{:S(2)}) collective-permute-start(bf16[256,512]{1,0:T(8,128)(2,1)S(1)} %collective-permute-done.2.refs_0_), channel_id=1, source_target_pairs={{0,1},{1,0},{2,3},{3,2},{4,5},{5,4},{6,7},{7,6},{8,9},{9,8},{10,11... | collective-permute-start | bytes 786440 | tf_op jit(solution)/shard_map/ppermute | solution.py:23
  31.8 14.4 %collective-permute-start.9 = (bf16[256,512]{1,0:T(8,128)(2,1)S(1)}, bf16[256,512]{1,0:T(8,128)(2,1)S(1)}, u32[]{:S(2)}, u32[]{:S(2)}) collective-permute-start(bf16[256,512]{1,0:T(8,128)(2,1)S(1)} %collective-permute-done.8.refs_0_), channel_id=1, source_target_pairs={{0,1},{1,0},{2,3},{3,2},{4,5},{5,4},{6,7},{7,6},{8,9},{9,8},{10,11... | collective-permute-start | bytes 786440 | tf_op jit(solution)/shard_map/ppermute | solution.py:23
  35.0 5.0 %collective-permute-start.14 = (bf16[128,512]{1,0:T(8,128)(2,1)S(1)}, bf16[128,512]{1,0:T(8,128)(2,1)S(1)}, u32[]{:S(2)}, u32[]{:S(2)}) collective-permute-start(bf16[128,512]{1,0:T(8,128)(2,1)S(1)} %collective-permute-done.12.refs_9_), channel_id=1, source_target_pairs={{0,2},{2,0},{4,6},{6,4},{8,10},{10,8},{12,14},{14,12},{16,18},{18,... | collective-permute-start | bytes 393224 | tf_op jit(solution)/shard_map/ppermute | solution.py:18
  40.0 9.6 %collective-permute-start.13 = (bf16[128,512]{1,0:T(8,128)(2,1)S(1)}, bf16[128,512]{1,0:T(8,128)(2,1)S(1)}, u32[]{:S(2)}, u32[]{:S(2)}) collective-permute-start(bf16[128,512]{1,0:T(8,128)(2,1)S(1)} %collective-permute-done.12.refs_9_), channel_id=1, source_target_pairs={{0,1},{1,0},{2,3},{3,2},{4,5},{5,4},{6,7},{7,6},{8,9},{9,8},{10,11... | collective-permute-start | bytes 393224 | tf_op jit(solution)/shard_map/ppermute | solution.py:23
  40.0 9.6 %collective-permute-start.11 = (bf16[128,512]{1,0:T(8,128)(2,1)S(1)}, bf16[128,512]{1,0:T(8,128)(2,1)S(1)}, u32[]{:S(2)}, u32[]{:S(2)}) collective-permute-start(bf16[128,512]{1,0:T(8,128)(2,1)S(1)} %collective-permute-done.10.refs_7_), channel_id=1, source_target_pairs={{0,1},{1,0},{2,3},{3,2},{4,5},{5,4},{6,7},{7,6},{8,9},{9,8},{10,11... | collective-permute-start | bytes 393224 | tf_op jit(solution)/shard_map/ppermute | solution.py:23
  40.5 10.5 %collective-permute-start.15 = (bf16[128,512]{1,0:T(8,128)(2,1)S(1)}, bf16[128,512]{1,0:T(8,128)(2,1)S(1)}, u32[]{:S(2)}, u32[]{:S(2)}) collective-permute-start(bf16[128,512]{1,0:T(8,128)(2,1)S(1)} %collective-permute-done.14.refs_7_), channel_id=1, source_target_pairs={{0,1},{1,0},{2,3},{3,2},{4,5},{5,4},{6,7},{7,6},{8,9},{9,8},{10,11... | collective-permute-start | bytes 393224 | tf_op jit(solution)/shard_map/ppermute | solution.py:23
  40.6 5.6 %collective-permute-start.7 = (s32[1,256]{1,0:T(1,128)}, s32[1,256]{1,0:T(1,128)S(1)}, u32[]{:S(2)}, u32[]{:S(2)}) collective-permute-start(s32[1,256]{1,0:T(1,128)} %sr_r.1), channel_id=1, source_target_pairs={{0,18},{2,16},{4,22},{6,20},{8,26},{10,24},{12,30},{14,28},{16,2},... | collective-permute-start | bytes 3080 | tf_op jit(solution)/shard_map/ppermute | solution.py:18
  47.7 1.9 %copy-start = (bf16[256,512]{1,0:T(8,128)(2,1)S(1)}, bf16[256,512]{1,0:T(8,128)(2,1)}, u32[]{:S(2)}) copy-start(bf16[256,512]{1,0:T(8,128)(2,1)} %cot_r.3) | copy-start | bytes 786436
  52.4 7.0 %collective-permute-start.16 = (bf16[32,512]{1,0:T(8,128)(2,1)S(1)}, bf16[32,512]{1,0:T(8,128)(2,1)S(1)}, u32[]{:S(2)}, u32[]{:S(2)}) collective-permute-start(bf16[32,512]{1,0:T(8,128)(2,1)S(1)} %get-tuple-element.83), channel_id=1, source_target_pairs={{0,4},{2,6},{4,0},{6,2},{8,12},{10,14},{12,8},{14,10},{16,20},{18,... | collective-permute-start | bytes 98312 | tf_op jit(solution)/shard_map/ppermute | solution.py:18
  54.0 5.9 %collective-permute-start.17 = (bf16[32,512]{1,0:T(8,128)(2,1)S(1)}, bf16[32,512]{1,0:T(8,128)(2,1)S(1)}, u32[]{:S(2)}, u32[]{:S(2)}) collective-permute-start(bf16[32,512]{1,0:T(8,128)(2,1)S(1)} %get-tuple-element.84), channel_id=1, source_target_pairs={{0,8},{2,10},{4,12},{6,14},{8,0},{10,2},{12,4},{14,6},{16,24},{18,... | collective-permute-start | bytes 98312 | tf_op jit(solution)/shard_map/ppermute | solution.py:18
  58.0 4.8 %collective-permute-start.18 = (bf16[32,512]{1,0:T(8,128)(2,1)S(1)}, bf16[32,512]{1,0:T(8,128)(2,1)S(1)}, u32[]{:S(2)}, u32[]{:S(2)}) collective-permute-start(bf16[32,512]{1,0:T(8,128)(2,1)S(1)} %get-tuple-element.85), channel_id=1, source_target_pairs={{0,12},{2,14},{4,8},{6,10},{8,4},{10,6},{12,0},{14,2},{16,28},{18,... | collective-permute-start | bytes 98312 | tf_op jit(solution)/shard_map/ppermute | solution.py:18

commit v3 on v2

--- a/solution.py
+++ b/solution.py
@@ -238,7 +238,7 @@
 
     def body(x12_r, sums_r, cp_r, pick_r, w_r, first_r, sr_r, *refs):
         got_r = refs[:layers]
-        first3_o, x3_s, mix_o, slope_o, x1_o, own3_o, near23_o, far13_o, back3_o, ac_s = (refs[layers], refs[-1], *refs[layers + 1 : -1])
+        first3_o, x3_s, mix_o, slope_o, x1_o, own3_o, near23_o, far13_o, ac_s = (refs[layers], refs[-1], *refs[layers + 1 : -1])
         seg = lax.axis_index("segment")
         for k in range(layers):
             at = piece_slice(seg, k, layers, piece)
@@ -251,9 +251,6 @@
         near23_o[0] = mm_nt(cp_r[1], picks[:, :bound]).astype(BF16)
         near23_o[1] = mm_nt(ac_s[:, :bound], pick_r[1]).astype(BF16)
         far13_o[1] = mm_nt(ac_s[:, bound:], pick_r[0]).astype(BF16)
-        back3_o[0] = mm_nt(pick_r[0], ac_s[:, bound:]).astype(BF16)
-        back3_o[1] = mm_nt(pick_r[1], ac_s[:, :bound]).astype(BF16)
-        back3_o[2] = own3_o[...].T
         for g in range(3):
             if g < 2:
                 agg = sums_r[g] + mm((far13_o, near23_o)[g][0], x3_s[...])
@@ -275,7 +272,6 @@
             sds((rows, rows), BF16),
             sds((2, rows, rows), BF16),
             sds((2, rows, rows), BF16),
-            sds((3, rows, rows), BF16),
         ),
         [(a, "v") for a in (x12, sums, cp, pick, w, first, diag_sr, *diag)],
         [pltpu.VMEM((rows, 2 * bound), BF16), pltpu.VMEM((rows, width), BF16)],
@@ -411,7 +407,7 @@
     m = len(arrays)
     last = layers - 1
 
-    def body(dps_r, sums_r, carry_r, mix_r, slope_r, mixn_r, slopen_r, later_mix_r, later_slope_r, w_r, back3_r, *refs):
+    def body(dps_r, sums_r, carry_r, mix_r, slope_r, mixn_r, slopen_r, later_mix_r, later_slope_r, w_r, *refs):
         own_at, near_at, far_at = readers(refs[:m])
         got_r = refs[m : m + layers]
         outs = refs[m + layers :]
@@ -430,7 +426,7 @@
         dpre = ((0.5 * up_s[3]).astype(F32) * later_slope_r[last - 1, 3]).astype(BF16)
         dpre_o[pl.ds(3 * rows, rows), :] = dpre
         dmix = dmix_of(dpre, w_r[last], last)
-        extra = (None, *[mm(back3_r[n], dmix) for n in range(3)])
+        extra = (None, mm_tn(far_at(3), dmix), mm_tn(near_at(3), dmix), mm_tn(own_at(3), dmix))
         for g in range(4):
             total = sums_r[g] if g == 0 else sums_r[g] + extra[g]
             up_s[g] = ((0.5 - 0.5 * SHARE) * total).astype(BF16)
@@ -487,7 +483,6 @@
                 later_mix,
                 later_slope,
                 w,
-                rest[7],
                 *arrays,
                 *diag,
             )

time: 63.7 us -> 63.6 us (level)
  no operation moved by 1% of the time
where the time goes in v3:
time: 63.6 us; the launch traced here: 63.4 us
  waiting for transfers between devices  31.1 us (49%)
  starting transfers between devices  19.1 us (30%)
  Pallas kernels  11.8 us (19%)
  between operations  0.74 us (1%)
  other arithmetic  0.65 us (1%)
    ppermute x12, waiting for transfers between devices, swapped(): lax.ppermute(x, 'dom', [(i, i ^ mask) for i in range(lax.axis_size('dom'))])  31 us
    ppermute x12, starting transfers between devices, swapped(): lax.ppermute(x, 'dom', [(i, i ^ mask) for i in range(lax.axis_size('dom'))])  18 us
    pallas_call x8, Pallas kernels, call(): pl.pallas_call(body, out_shape=tuple(out_shape), in_specs=specs, out_spec...  11.8 us
  transfers between devices with their start and end apart: 19, of which 8 were waited for; matrix products, arithmetic and copies ran while one was open for 0% of the time, Pallas kernels for 15%

profile of v3, /device:TPU:0, one launch (start us, length us, event | category | flops | bytes accessed | tf_op | source)
XLA Modules:
  0.0 63.4 jit_solution(3323571600061585316)
XLA Ops:
  0.6 1.1 %shard_map.86 = (bf16[256,512]{1,0:T(8,128)(2,1)S(1)}, bf16[128,512]{1,0:T(8,128)(2,1)S(1)}) custom-call(bf16[256,512]{1,0:T(8,128)(2,1)} %feats_r.3, bf16[256,256]{1,0:T(8,128)(2,1)} %adj_r.3, bf16[256,256]{1,0:T(8,128)(2,1)} %couple_r.3, bf16[256,512]{1,0:T(8,128)(2,1)} %cot_r.3), custom_call_target="tpu_custom_call" | custom-call | tf_op jit(solution)/shard_map/pallas_call | solution.py:60
  1.7 4.1 %collective-permute-start.4 = (bf16[256,512]{1,0:T(8,128)(2,1)S(1)}, bf16[256,512]{1,0:T(8,128)(2,1)S(1)}, u32[]{:S(2)}, u32[]{:S(2)}) collective-permute-start(bf16[256,512]{1,0:T(8,128)(2,1)S(1)} %get-tuple-element.48), channel_id=1, source_target_pairs={{0,16},{2,18},{4,20},{6,22},{8,24},{10,26},{12,28},{14,30},{16,0},... | collective-permute-start | bytes 786440 | tf_op jit(solution)/shard_map/ppermute | solution.py:18
  5.9 1.5 %collective-permute-start.2 = (bf16[256,512]{1,0:T(8,128)(2,1)S(1)}, bf16[256,512]{1,0:T(8,128)(2,1)S(1)}, u32[]{:S(2)}, u32[]{:S(2)}) collective-permute-start(bf16[256,512]{1,0:T(8,128)(2,1)S(1)} %get-tuple-element.48), channel_id=1, source_target_pairs={{0,2},{2,0},{4,6},{6,4},{8,10},{10,8},{12,14},{14,12},{16,18},{18,... | collective-permute-start | bytes 786440 | tf_op jit(solution)/shard_map/ppermute | solution.py:18
  7.3 10.4 %collective-permute-done.4.refs_2_ = bf16[256,512]{1,0:T(8,128)(2,1)S(1)} collective-permute-done((bf16[256,512]{1,0:T(8,128)(2,1)S(1)}, bf16[256,512]{1,0:T(8,128)(2,1)S(1)}, u32[]{:S(2)}, u32[]{:S(2)}) %collective-permute-start.4) | collective-permute-done | bytes 262176 | tf_op jit(solution)/shard_map/ppermute | solution.py:18
  17.8 1.5 %collective-permute-start.8 = (bf16[256,512]{1,0:T(8,128)(2,1)S(1)}, bf16[256,512]{1,0:T(8,128)(2,1)S(1)}, u32[]{:S(2)}, u32[]{:S(2)}) collective-permute-start(bf16[256,512]{1,0:T(8,128)(2,1)S(1)} %collective-permute-done.4.refs_2_), channel_id=1, source_target_pairs={{0,2},{2,0},{4,6},{6,4},{8,10},{10,8},{12,14},{14,12},{16,18},{18,... | collective-permute-start | bytes 786440 | tf_op jit(solution)/shard_map/ppermute | solution.py:18
  19.3 0.5 collective-permute-start
  19.8 5.5 %collective-permute-done.near_sr_r = s32[1,256]{1,0:T(1,128)S(1)} collective-permute-done((s32[1,256]{1,0:T(1,128)}, s32[1,256]{1,0:T(1,128)S(1)}, u32[]{:S(2)}, u32[]{:S(2)}) %collective-permute-start) | collective-permute-done | bytes 1056 | tf_op jit(solution)/shard_map/ppermute | solution.py:18
  25.3 0.7 %collective-permute-start.1 = (s32[1,256]{1,0:T(1,128)}, s32[1,256]{1,0:T(1,128)S(1)}, u32[]{:S(2)}, u32[]{:S(2)}) collective-permute-start(s32[1,256]{1,0:T(1,128)} %sr_r.1), channel_id=1, source_target_pairs={{0,16},{2,18},{4,20},{6,22},{8,24},{10,26},{12,28},{14,30},{16,0},... | collective-permute-start | bytes 3080 | tf_op jit(solution)/shard_map/ppermute | solution.py:18
  26.0 4.0 %collective-permute-done.1.far_sr_r = s32[1,256]{1,0:T(1,128)S(1)} collective-permute-done((s32[1,256]{1,0:T(1,128)}, s32[1,256]{1,0:T(1,128)S(1)}, u32[]{:S(2)}, u32[]{:S(2)}) %collective-permute-start.1) | collective-permute-done | bytes 1056 | tf_op jit(solution)/shard_map/ppermute | solution.py:18
  30.0 1.3 %collective-permute-start.10 = (bf16[128,512]{1,0:T(8,128)(2,1)S(1)}, bf16[128,512]{1,0:T(8,128)(2,1)S(1)}, u32[]{:S(2)}, u32[]{:S(2)}) collective-permute-start(bf16[128,512]{1,0:T(8,128)(2,1)S(1)} %get-tuple-element.67), channel_id=1, source_target_pairs={{0,2},{2,0},{4,6},{6,4},{8,10},{10,8},{12,14},{14,12},{16,18},{18,... | collective-permute-start | bytes 393224 | tf_op jit(solution)/shard_map/ppermute | solution.py:18
  31.3 0.5 collective-permute-start.3
  31.8 0.1 collective-permute-start.9
  31.9 3.1 %collective-permute-done.10.refs_7_ = bf16[128,512]{1,0:T(8,128)(2,1)S(1)} collective-permute-done((bf16[128,512]{1,0:T(8,128)(2,1)S(1)}, bf16[128,512]{1,0:T(8,128)(2,1)S(1)}, u32[]{:S(2)}, u32[]{:S(2)}) %collective-permute-start.10) | collective-permute-done | bytes 131104 | tf_op jit(solution)/shard_map/ppermute | solution.py:18
  35.0 1.8 %collective-permute-start.14 = (bf16[128,512]{1,0:T(8,128)(2,1)S(1)}, bf16[128,512]{1,0:T(8,128)(2,1)S(1)}, u32[]{:S(2)}, u32[]{:S(2)}) collective-permute-start(bf16[128,512]{1,0:T(8,128)(2,1)S(1)} %collective-permute-done.12.refs_9_), channel_id=1, source_target_pairs={{0,2},{2,0},{4,6},{6,4},{8,10},{10,8},{12,14},{14,12},{16,18},{18,... | collective-permute-start | bytes 393224 | tf_op jit(solution)/shard_map/ppermute | solution.py:18
  36.8 3.1 %collective-permute-done.14.refs_7_ = bf16[128,512]{1,0:T(8,128)(2,1)S(1)} collective-permute-done((bf16[128,512]{1,0:T(8,128)(2,1)S(1)}, bf16[128,512]{1,0:T(8,128)(2,1)S(1)}, u32[]{:S(2)}, u32[]{:S(2)}) %collective-permute-start.14) | collective-permute-done | bytes 131104 | tf_op jit(solution)/shard_map/ppermute | solution.py:18
  40.0 0.5 collective-permute-start.11
  40.5 0.1 collective-permute-start.15
  40.6 0.9 %collective-permute-start.7 = (s32[1,256]{1,0:T(1,128)}, s32[1,256]{1,0:T(1,128)S(1)}, u32[]{:S(2)}, u32[]{:S(2)}) collective-permute-start(s32[1,256]{1,0:T(1,128)} %sr_r.1), channel_id=1, source_target_pairs={{0,18},{2,16},{4,22},{6,20},{8,26},{10,24},{12,30},{14,28},{16,2},... | collective-permute-start | bytes 3080 | tf_op jit(solution)/shard_map/ppermute | solution.py:18
  41.4 1.3 %shard_map.85 = (bf16[256,512]{1,0:T(8,128)(2,1)S(1)}, bf16[256,256]{1,0:T(8,128)(2,1)S(1)}, bf16[256,256]{1,0:T(8,128)(2,1)S(1)}, bf16[256,256]{1,0:T(8,128)(2,1)S(1)}, f32[256,512]{1,0:T(8,128)S(1)}) custom-call(bf16[256,512]{1,0:T(8,128)(2,1)} %feats_r.3, bf16[256,256]{1,0:T(8,128)(2,1)} %adj_r.3, bf16[256,256]{1,0:T(8,128)(2,1)} %couple_r.3, s32[1,256]{1,0:T(1,128)} %sr_r.1), custom_call_target="tpu_custom_call" | custom-call | tf_op jit(solution)/shard_map/pallas_call | solution.py:60
  42.8 1.9 %shard_map.87 = (bf16[2,256,512]{2,1,0:T(8,128)(2,1)S(1)}, bf16[256,512]{1,0:T(8,128)(2,1)S(1)}, f32[256,512]{1,0:T(8,128)S(1)}, bf16[256,512]{1,0:T(8,128)(2,1)...) custom-call(bf16[256,512]{1,0:T(8,128)(2,1)S(1)} %get-tuple-element., ...), custom_call_target="tpu_custom_call" | custom-call | tf_op jit(solution)/shard_map/pallas_call | solution.py:60
  44.7 1.5 %collective-permute-done.7.sr_r = s32[1,256]{1,0:T(1,128)S(1)} collective-permute-done((s32[1,256]{1,0:T(1,128)}, s32[1,256]{1,0:T(1,128)S(1)}, u32[]{:S(2)}, u32[]{:S(2)}) %collective-permute-start.7) | collective-permute-done | bytes 1056 | tf_op jit(solution)/shard_map/ppermute | solution.py:18
  46.2 1.4 %shard_map.88 = (f32[256,512]{1,0:T(8,128)S(1)}, bf16[3,256,512]{2,1,0:T(8,128)(2,1)S(1)}, f32[3,256,512]{2,1,0:T(8,128)S(1)}, bf16[3,256,512]{2,1,0:T(8,128)(2,...) custom-call(bf16[2,256,512]{2,1,0:T(8,128)(2,1)S(1)} %get-tuple-element.51., ...), custom_call_target="tpu_custom_call" | custom-call | tf_op jit(solution)/shard_map/pallas_call | solution.py:60
  47.6 0.0 copy-start
  47.6 1.9 %shard_map.89 = (bf16[256,512]{1,0:T(8,128)(2,1)S(1)}, bf16[1,4,256,512]{3,2,1,0:T(8,128)(2,1)S(1)}, f32[1,4,256,512]{3,2,1,0:T(8,128)S(1)}) custom-call(f32[3,256,512]{2,1,0:T(8,128)S(1)} %get-tuple-element.50.first_r, f32[256,512]{1,0:T(8,128)S(1)} %get-tuple-element.56.first3_r, bf16[256,512]{1,0:T(8,128)(2,1)S(1)} %get-tuple-element.57.x1_r, ...), custom_call_target="tpu_custom_call" | custom-call | tf_op jit(solution)/shard_map/pallas_call | solution.py:60
  49.5 1.4 %shard_map.90 = (bf16[768,512]{1,0:T(8,128)(2,1)S(1)}, f32[4,256,512]{2,1,0:T(8,128)S(1)}, f32[256,512]{1,0:T(8,128)S(1)}) custom-call(bf16[256,512]{1,0:T(8,128)(2,1)S(1)} %copy-done, bf16[2,512,512]{2,1,0:T(8,128)(2,1)S(1)} %get-tuple-element.49.w_r, f32[1,4,256,512]{3,2,1,0:T(8,128)S(1)} %get-tuple-element.66.slope_r.later_slope_r, ...), custom_call_target="tpu_custom_call" | custom-call | tf_op jit(solution)/shard_map/pallas_call | solution.py:60
  50.9 1.4 %shard_map.91 = (bf16[1024,512]{1,0:T(8,128)(2,1)S(1)}, f32[256,512]{1,0:T(8,128)S(1)}, f32[32,512]{1,0:T(8,128)S(1)}, bf16[32,512]{1,0:T(8,128)(2,1)S(1)}, bf16...) custom-call(bf16[768,512]{1,0:T(8,128)(2,1)S(1)} %get-tuple-element.68.dps_r, ...), custom_call_target="tpu_custom_call" | custom-call | tf_op jit(solution)/shard_map/pallas_call | solution.py:60
  52.4 1.6 %collective-permute-start.16 = (bf16[32,512]{1,0:T(8,128)(2,1)S(1)}, bf16[32,512]{1,0:T(8,128)(2,1)S(1)}, u32[]{:S(2)}, u32[]{:S(2)}) collective-permute-start(bf16[32,512]{1,0:T(8,128)(2,1)S(1)} %get-tuple-element.81), channel_id=1, source_target_pairs={{0,4},{2,6},{4,0},{6,2},{8,12},{10,14},{12,8},{14,10},{16,20},{18,... | collective-permute-start | bytes 98312 | tf_op jit(solution)/shard_map/ppermute | solution.py:18
  53.9 4.0 %collective-permute-start.17 = (bf16[32,512]{1,0:T(8,128)(2,1)S(1)}, bf16[32,512]{1,0:T(8,128)(2,1)S(1)}, u32[]{:S(2)}, u32[]{:S(2)}) collective-permute-start(bf16[32,512]{1,0:T(8,128)(2,1)S(1)} %get-tuple-element.82), channel_id=1, source_target_pairs={{0,8},{2,10},{4,12},{6,14},{8,0},{10,2},{12,4},{14,6},{16,24},{18,... | collective-permute-start | bytes 98312 | tf_op jit(solution)/shard_map/ppermute | solution.py:18
  58.0 1.4 %shard_map.92 = (f32[256,256]{1,0:T(8,128)}, bf16[256,512]{1,0:T(8,128)(2,1)}) custom-call(bf16[1024,512]{1,0:T(8,128)(2,1)S(1)} %get-tuple-element.76.dpre_r, f32[256,512]{1,0:T(8,128)S(1)} %get-tuple-element.77.carry_r, bf16[2,512,512]{2,1,0:T(8,128)(2,1)S(1)} %get-tuple-element.49.w_r, bf16[256,512]{1,0:T(8,128)(2,1)S(1)} %get-tuple-element.78.acts_r, ...), custom_call_target="tpu_custom_call" | custom-call | tf_op jit(solution)/shard_map/pallas_call | solution.py:60
  59.4 0.5 collective-permute-done.17
  59.8 2.9 %collective-permute-done.18 = bf16[32,512]{1,0:T(8,128)(2,1)S(1)} collective-permute-done((bf16[32,512]{1,0:T(8,128)(2,1)S(1)}, bf16[32,512]{1,0:T(8,128)(2,1)S(1)}, u32[]{:S(2)}, u32[]{:S(2)}) %collective-permute-start.18) | collective-permute-done | bytes 32800 | tf_op jit(solution)/shard_map/ppermute | solution.py:18
  62.8 0.6 %add_bitcast_fusion = f32[1,32,512]{2,1,0:T(8,128)} fusion(bf16[32,512]{1,0:T(8,128)(2,1)S(1)} %collective-permute-done.18, bf16[32,512]{1,0:T(8,128)(2,1)S(1)} %collective-permute-done.17, f32[32,512]{1,0:T(8,128)S(1)} %get-tuple-element.80, bf16[32,512]{1,0:T(8,128)(2,1)S(1)} %collective-permute-done.16), kind=kLoop, calls=%fused_computation | loop fusion | flops 98304 | bytes 229376 | tf_op jit(solution)/shard_map/broadcast_in_dim | solution.py:569
  (17 shorter events, 0.0 us)
Async XLA Ops:
  1.7 16.1 %collective-permute-start.4 = (bf16[256,512]{1,0:T(8,128)(2,1)S(1)}, bf16[256,512]{1,0:T(8,128)(2,1)S(1)}, u32[]{:S(2)}, u32[]{:S(2)}) collective-permute-start(bf16[256,512]{1,0:T(8,128)(2,1)S(1)} %get-tuple-element.48), channel_id=1, source_target_pairs={{0,16},{2,18},{4,20},{6,22},{8,24},{10,26},{12,28},{14,30},{16,0},... | collective-permute-start | bytes 786440 | tf_op jit(solution)/shard_map/ppermute | solution.py:18
  5.9 25.4 %collective-permute-start.2 = (bf16[256,512]{1,0:T(8,128)(2,1)S(1)}, bf16[256,512]{1,0:T(8,128)(2,1)S(1)}, u32[]{:S(2)}, u32[]{:S(2)}) collective-permute-start(bf16[256,512]{1,0:T(8,128)(2,1)S(1)} %get-tuple-element.48), channel_id=1, source_target_pairs={{0,2},{2,0},{4,6},{6,4},{8,10},{10,8},{12,14},{14,12},{16,18},{18,... | collective-permute-start | bytes 786440 | tf_op jit(solution)/shard_map/ppermute | solution.py:18
  7.3 33.2 %collective-permute-start.6 = (bf16[512,512]{1,0:T(8,128)(2,1)}, bf16[512,512]{1,0:T(8,128)(2,1)S(1)}, u32[]{:S(2)}, u32[]{:S(2)}) collective-permute-start(bf16[512,512]{1,0:T(8,128)(2,1)} %refs_4_.1), channel_id=1, source_target_pairs={{0,1},{1,0},{2,3},{3,2},{4,5},{5,4},{6,7},{7,6},{8,9},{9,8},{10,11... | collective-permute-start | bytes 1572872 | tf_op jit(solution)/shard_map/ppermute | solution.py:23
  17.8 14.0 %collective-permute-start.8 = (bf16[256,512]{1,0:T(8,128)(2,1)S(1)}, bf16[256,512]{1,0:T(8,128)(2,1)S(1)}, u32[]{:S(2)}, u32[]{:S(2)}) collective-permute-start(bf16[256,512]{1,0:T(8,128)(2,1)S(1)} %collective-permute-done.4.refs_2_), channel_id=1, source_target_pairs={{0,2},{2,0},{4,6},{6,4},{8,10},{10,8},{12,14},{14,12},{16,18},{18,... | collective-permute-start | bytes 786440 | tf_op jit(solution)/shard_map/ppermute | solution.py:18
  19.3 12.0 %collective-permute-start.12 = (bf16[128,512]{1,0:T(8,128)(2,1)S(1)}, bf16[128,512]{1,0:T(8,128)(2,1)S(1)}, u32[]{:S(2)}, u32[]{:S(2)}) collective-permute-start(bf16[128,512]{1,0:T(8,128)(2,1)S(1)} %get-tuple-element.67), channel_id=1, source_target_pairs={{0,16},{2,18},{4,20},{6,22},{8,24},{10,26},{12,28},{14,30},{16,0},... | collective-permute-start | bytes 393224 | tf_op jit(solution)/shard_map/ppermute | solution.py:18
  19.3 6.0 %collective-permute-start = (s32[1,256]{1,0:T(1,128)}, s32[1,256]{1,0:T(1,128)S(1)}, u32[]{:S(2)}, u32[]{:S(2)}) collective-permute-start(s32[1,256]{1,0:T(1,128)} %sr_r.1), channel_id=1, source_target_pairs={{0,2},{2,0},{4,6},{6,4},{8,10},{10,8},{12,14},{14,12},{16,18},{18,... | collective-permute-start | bytes 3080 | tf_op jit(solution)/shard_map/ppermute | solution.py:18
  25.3 4.7 %collective-permute-start.1 = (s32[1,256]{1,0:T(1,128)}, s32[1,256]{1,0:T(1,128)S(1)}, u32[]{:S(2)}, u32[]{:S(2)}) collective-permute-start(s32[1,256]{1,0:T(1,128)} %sr_r.1), channel_id=1, source_target_pairs={{0,16},{2,18},{4,20},{6,22},{8,24},{10,26},{12,28},{14,30},{16,0},... | collective-permute-start | bytes 3080 | tf_op jit(solution)/shard_map/ppermute | solution.py:18
  30.0 5.0 %collective-permute-start.10 = (bf16[128,512]{1,0:T(8,128)(2,1)S(1)}, bf16[128,512]{1,0:T(8,128)(2,1)S(1)}, u32[]{:S(2)}, u32[]{:S(2)}) collective-permute-start(bf16[128,512]{1,0:T(8,128)(2,1)S(1)} %get-tuple-element.67), channel_id=1, source_target_pairs={{0,2},{2,0},{4,6},{6,4},{8,10},{10,8},{12,14},{14,12},{16,18},{18,... | collective-permute-start | bytes 393224 | tf_op jit(solution)/shard_map/ppermute | solution.py:18
  31.3 8.7 %collective-permute-start.5 = (bf16[256,512]{1,0:T(8,128)(2,1)S(1)}, bf16[256,512]{1,0:T(8,128)(2,1)S(1)}, u32[]{:S(2)}, u32[]{:S(2)}) collective-permute-start(bf16[256,512]{1,0:T(8,128)(2,1)S(1)} %collective-permute-done.4.refs_2_), channel_id=1, source_target_pairs={{0,1},{1,0},{2,3},{3,2},{4,5},{5,4},{6,7},{7,6},{8,9},{9,8},{10,11... | collective-permute-start | bytes 786440 | tf_op jit(solution)/shard_map/ppermute | solution.py:23
  31.3 9.2 %collective-permute-start.3 = (bf16[256,512]{1,0:T(8,128)(2,1)S(1)}, bf16[256,512]{1,0:T(8,128)(2,1)S(1)}, u32[]{:S(2)}, u32[]{:S(2)}) collective-permute-start(bf16[256,512]{1,0:T(8,128)(2,1)S(1)} %collective-permute-done.2.refs_0_), channel_id=1, source_target_pairs={{0,1},{1,0},{2,3},{3,2},{4,5},{5,4},{6,7},{7,6},{8,9},{9,8},{10,11... | collective-permute-start | bytes 786440 | tf_op jit(solution)/shard_map/ppermute | solution.py:23
  31.8 14.4 %collective-permute-start.9 = (bf16[256,512]{1,0:T(8,128)(2,1)S(1)}, bf16[256,512]{1,0:T(8,128)(2,1)S(1)}, u32[]{:S(2)}, u32[]{:S(2)}) collective-permute-start(bf16[256,512]{1,0:T(8,128)(2,1)S(1)} %collective-permute-done.8.refs_0_), channel_id=1, source_target_pairs={{0,1},{1,0},{2,3},{3,2},{4,5},{5,4},{6,7},{7,6},{8,9},{9,8},{10,11... | collective-permute-start | bytes 786440 | tf_op jit(solution)/shard_map/ppermute | solution.py:23
  35.0 5.0 %collective-permute-start.14 = (bf16[128,512]{1,0:T(8,128)(2,1)S(1)}, bf16[128,512]{1,0:T(8,128)(2,1)S(1)}, u32[]{:S(2)}, u32[]{:S(2)}) collective-permute-start(bf16[128,512]{1,0:T(8,128)(2,1)S(1)} %collective-permute-done.12.refs_9_), channel_id=1, source_target_pairs={{0,2},{2,0},{4,6},{6,4},{8,10},{10,8},{12,14},{14,12},{16,18},{18,... | collective-permute-start | bytes 393224 | tf_op jit(solution)/shard_map/ppermute | solution.py:18
  40.0 9.5 %collective-permute-start.13 = (bf16[128,512]{1,0:T(8,128)(2,1)S(1)}, bf16[128,512]{1,0:T(8,128)(2,1)S(1)}, u32[]{:S(2)}, u32[]{:S(2)}) collective-permute-start(bf16[128,512]{1,0:T(8,128)(2,1)S(1)} %collective-permute-done.12.refs_9_), channel_id=1, source_target_pairs={{0,1},{1,0},{2,3},{3,2},{4,5},{5,4},{6,7},{7,6},{8,9},{9,8},{10,11... | collective-permute-start | bytes 393224 | tf_op jit(solution)/shard_map/ppermute | solution.py:23
  40.0 9.5 %collective-permute-start.11 = (bf16[128,512]{1,0:T(8,128)(2,1)S(1)}, bf16[128,512]{1,0:T(8,128)(2,1)S(1)}, u32[]{:S(2)}, u32[]{:S(2)}) collective-permute-start(bf16[128,512]{1,0:T(8,128)(2,1)S(1)} %collective-permute-done.10.refs_7_), channel_id=1, source_target_pairs={{0,1},{1,0},{2,3},{3,2},{4,5},{5,4},{6,7},{7,6},{8,9},{9,8},{10,11... | collective-permute-start | bytes 393224 | tf_op jit(solution)/shard_map/ppermute | solution.py:23
  40.5 10.4 %collective-permute-start.15 = (bf16[128,512]{1,0:T(8,128)(2,1)S(1)}, bf16[128,512]{1,0:T(8,128)(2,1)S(1)}, u32[]{:S(2)}, u32[]{:S(2)}) collective-permute-start(bf16[128,512]{1,0:T(8,128)(2,1)S(1)} %collective-permute-done.14.refs_7_), channel_id=1, source_target_pairs={{0,1},{1,0},{2,3},{3,2},{4,5},{5,4},{6,7},{7,6},{8,9},{9,8},{10,11... | collective-permute-start | bytes 393224 | tf_op jit(solution)/shard_map/ppermute | solution.py:23
  40.6 5.6 %collective-permute-start.7 = (s32[1,256]{1,0:T(1,128)}, s32[1,256]{1,0:T(1,128)S(1)}, u32[]{:S(2)}, u32[]{:S(2)}) collective-permute-start(s32[1,256]{1,0:T(1,128)} %sr_r.1), channel_id=1, source_target_pairs={{0,18},{2,16},{4,22},{6,20},{8,26},{10,24},{12,30},{14,28},{16,2},... | collective-permute-start | bytes 3080 | tf_op jit(solution)/shard_map/ppermute | solution.py:18
  47.6 1.9 %copy-start = (bf16[256,512]{1,0:T(8,128)(2,1)S(1)}, bf16[256,512]{1,0:T(8,128)(2,1)}, u32[]{:S(2)}) copy-start(bf16[256,512]{1,0:T(8,128)(2,1)} %cot_r.3) | copy-start | bytes 786436
  52.4 7.0 %collective-permute-start.16 = (bf16[32,512]{1,0:T(8,128)(2,1)S(1)}, bf16[32,512]{1,0:T(8,128)(2,1)S(1)}, u32[]{:S(2)}, u32[]{:S(2)}) collective-permute-start(bf16[32,512]{1,0:T(8,128)(2,1)S(1)} %get-tuple-element.81), channel_id=1, source_target_pairs={{0,4},{2,6},{4,0},{6,2},{8,12},{10,14},{12,8},{14,10},{16,20},{18,... | collective-permute-start | bytes 98312 | tf_op jit(solution)/shard_map/ppermute | solution.py:18
  53.9 5.9 %collective-permute-start.17 = (bf16[32,512]{1,0:T(8,128)(2,1)S(1)}, bf16[32,512]{1,0:T(8,128)(2,1)S(1)}, u32[]{:S(2)}, u32[]{:S(2)}) collective-permute-start(bf16[32,512]{1,0:T(8,128)(2,1)S(1)} %get-tuple-element.82), channel_id=1, source_target_pairs={{0,8},{2,10},{4,12},{6,14},{8,0},{10,2},{12,4},{14,6},{16,24},{18,... | collective-permute-start | bytes 98312 | tf_op jit(solution)/shard_map/ppermute | solution.py:18
  58.0 4.8 %collective-permute-start.18 = (bf16[32,512]{1,0:T(8,128)(2,1)S(1)}, bf16[32,512]{1,0:T(8,128)(2,1)S(1)}, u32[]{:S(2)}, u32[]{:S(2)}) collective-permute-start(bf16[32,512]{1,0:T(8,128)(2,1)S(1)} %get-tuple-element.83), channel_id=1, source_target_pairs={{0,12},{2,14},{4,8},{6,10},{8,4},{10,6},{12,0},{14,2},{16,28},{18,... | collective-permute-start | bytes 98312 | tf_op jit(solution)/shard_map/ppermute | solution.py:18
